TPU v7x, 512 devices: a whole 4x4x16 slice. The times are simulated.
512 devices in a mesh: dp: 8 (over y, core), expert: 64 (over z, x).
Axes of the slice: x: 4, y: 4, z: 16, core: 2. Of those that a mesh axis runs over, the one named last changes fastest.
Arguments:
- tokens: bfloat16 [16384, 2048], P(('dp', 'expert')), may hold values from -6 to 6
- route_weight: float32 [16384, 8], P(('dp', 'expert')), may hold values from 0.03 to 0.4
- upstream: bfloat16 [16384, 2048], P(('dp', 'expert')), may hold values from -6 to 6
- expert_index: int32 [16384, 8], P(('dp', 'expert')), may hold values from 0 to 63, all different within a row; in each aligned block of 32 rows (0 to 31, 32 to 63, ...) at most 5 rows name the same one
- gate_weight: bfloat16 [64, 2048, 768], P('expert', 'dp'), may hold values from -0.125 to 0.125
- up_weight: bfloat16 [64, 2048, 768], P('expert', 'dp'), may hold values from -0.125 to 0.125
- down_weight: bfloat16 [64, 2048, 768], P('expert', 'dp'), may hold values from -0.21875 to 0.21875
Outputs:
- combined: bfloat16 [16384, 2048], P(('dp', 'expert'))
- token_grad: bfloat16 [16384, 2048], P(('dp', 'expert'))
- route_grad: float32 [16384, 8], P(('dp', 'expert'))
- down_grad: bfloat16 [64, 2048, 768], P('expert', 'dp')
Inputs may be any that keep to these rules, and one draw needn't show every extreme that they name: `expert_index`: each row names 8 different experts. Among the rows of one device no expert is named more than 5 times, and in every draw some device names some expert exactly 5 times.
All inputs are finite; a program needn't handle non-finite values.
Results may differ from a plain program's by a relative error of at most 0.017.
Values may be sent and summed in bfloat16 or wider, within the bound.
A program may use at most 128 MiB of HBM per device.

v0:
```python
import jax
import jax.numpy as jnp
from jax import lax
from jax.sharding import PartitionSpec as P


def silu_parts(gate_value):
    sigmoid_value = jax.nn.sigmoid(gate_value)
    return (gate_value * sigmoid_value, sigmoid_value * (1.0 + gate_value * (1.0 - sigmoid_value)))


def contract_last(left, right):
    return lax.dot_general(
        left, right, (((1,), (1,)), ((), ())), preferred_element_type=jnp.float32
    )


def contract_first(left, right):
    return lax.dot_general(
        left, right, (((0,), (0,)), ((), ())), preferred_element_type=jnp.float32
    )


def on_device(tokens, route_weight, upstream, expert_index, gate_weight, up_weight, down_weight):
    n_experts = lax.axis_size("expert")
    tok_count, top_count = expert_index.shape
    model_width = tokens.shape[1]
    assignments = tok_count * top_count
    capacity = max(2, (5 * assignments + 4 * n_experts - 1) // (4 * n_experts))
    slot_total = n_experts * capacity
    flat_ids = expert_index.reshape(assignments)
    onehot = (flat_ids[:, None] == jnp.arange(n_experts, dtype=jnp.int32)[None, :]).astype(
        jnp.int32
    )
    earlier = jnp.cumsum(onehot, axis=0) - onehot
    position = flat_ids * capacity + jnp.sum(earlier * onehot, axis=1)
    selector = position[None, :] == jnp.arange(slot_total, dtype=jnp.int32)[:, None]
    select_rows = selector.astype(jnp.bfloat16)
    select_tokens = (
        selector.reshape(slot_total, tok_count, top_count).any(axis=2).astype(jnp.bfloat16)
    )
    send_tokens = jnp.dot(select_tokens, tokens, preferred_element_type=jnp.float32).astype(
        jnp.bfloat16
    )
    send_tokens = send_tokens.reshape(n_experts, capacity, model_width)
    grad_rows = (route_weight[:, :, None] * upstream[:, None, :].astype(jnp.float32)).astype(
        jnp.bfloat16
    )
    grad_rows = grad_rows.reshape(assignments, model_width)
    send_grads = jnp.dot(select_rows, grad_rows, preferred_element_type=jnp.float32).astype(
        jnp.bfloat16
    )
    send_grads = send_grads.reshape(n_experts, capacity, model_width)
    routed_tokens, routed_grads = (
        lax.all_to_all(send_tokens, "expert", split_axis=0, concat_axis=0, tiled=True),
        lax.all_to_all(send_grads, "expert", split_axis=0, concat_axis=0, tiled=True),
    )
    routed_tokens = routed_tokens.reshape(slot_total, model_width)
    gathered = (
        lax.all_gather(gate_weight, "dp", axis=1, tiled=True),
        lax.all_gather(up_weight, "dp", axis=1, tiled=True),
        lax.all_gather(down_weight, "dp", axis=1, tiled=True),
    )
    w_gate, w_up, w_down = (gathered[0][0], gathered[1][0], gathered[2][0])
    gate_value = jnp.dot(routed_tokens, w_gate, preferred_element_type=jnp.float32)
    up_value = jnp.dot(routed_tokens, w_up, preferred_element_type=jnp.float32)
    activated, slope_value = silu_parts(gate_value)
    hidden = (activated * up_value).astype(jnp.bfloat16)
    expert_out = contract_last(hidden, w_down).astype(jnp.bfloat16)
    returned = lax.all_to_all(
        expert_out.reshape(n_experts, capacity, model_width),
        "expert",
        split_axis=0,
        concat_axis=0,
        tiled=True,
    )
    out_rows = contract_first(select_rows, returned.reshape(slot_total, model_width))
    out_rows = out_rows.reshape(tok_count, top_count, model_width)
    combined = jnp.sum(route_weight[:, :, None] * out_rows, axis=1).astype(jnp.bfloat16)
    route_grad = jnp.sum(out_rows * upstream[:, None, :].astype(jnp.float32), axis=2)
    routed_grads = routed_grads.reshape(slot_total, model_width)
    hidden_grad = jnp.dot(routed_grads, w_down, preferred_element_type=jnp.float32)
    down_grad = lax.psum_scatter(
        contract_first(routed_grads, hidden).astype(jnp.bfloat16),
        "dp",
        scatter_dimension=0,
        tiled=True,
    )[None]
    gate_grad = (hidden_grad * up_value * slope_value).astype(jnp.bfloat16)
    up_grad = (hidden_grad * activated).astype(jnp.bfloat16)
    row_grad = (contract_last(gate_grad, w_gate) + contract_last(up_grad, w_up)).astype(
        jnp.bfloat16
    )
    returned_grads = lax.all_to_all(
        row_grad.reshape(n_experts, capacity, model_width),
        "expert",
        split_axis=0,
        concat_axis=0,
        tiled=True,
    )
    token_grad = contract_first(
        select_tokens, returned_grads.reshape(slot_total, model_width)
    ).astype(jnp.bfloat16)
    return (combined, token_grad, route_grad, down_grad)


def solution(mesh):
    return jax.shard_map(
        on_device,
        mesh=mesh,
        in_specs=(
            P(("dp", "expert"), None),
            P(("dp", "expert"), None),
            P(("dp", "expert"), None),
            P(("dp", "expert"), None),
            P("expert", "dp", None),
            P("expert", "dp", None),
            P("expert", "dp", None),
        ),
        out_specs=(
            P(("dp", "expert"), None),
            P(("dp", "expert"), None),
            P(("dp", "expert"), None),
            P("expert", "dp", None),
        ),
        check_vma=False,
    )
```

profile of v0, /device:TPU:24, one launch (start us, length us, event | category | flops | bytes accessed | tf_op | source)
XLA Modules:
  0.0 461.1 jit_solution(18187432493527867307)
XLA Ops:
  7.2 0.7 all-gather.4.cloned.1.call-update
  8.0 0.7 all-gather.6.cloned.1.call-update
  8.7 0.8 copy.28
  9.4 0.1 reshape.95
  9.5 0.1 eq.65
  9.6 0.6 reduce-window.6
  10.2 0.2 slice_reduce_fusion
  10.5 0.1 fusion.36
  10.6 0.1 reduce_sum.30
  10.7 0.6 copy-done.4
  11.3 0.2 fusion.30
  11.5 0.5 convolution_convert_fusion.2
  12.0 1.7 reshape.97
  13.7 18.7 %all-to-all-start = ((bf16[64,5,2048]{2,1,0:T(8,128)(2,1)}), bf16[64,5,2048]{2,1,0:T(8,128)(2,1)S(1)}, u32[]{:S(2)}, u32[]{:S(2)}) async-start(bf16[64,5,2048]{2,1,0:T(8,128)(2,1)} %reshape.97), calls=%async_computation | async-start | bytes 4194304 | tf_op jit(solution)/shard_map/all_to_all | solution.py:55
  32.5 0.7 all-gather.8.cloned.1.call-update
  33.2 0.7 convert_element_type.54
  34.0 0.1 mul.81
  34.1 0.5 copy-done.5
  34.6 1.5 convolution_convert_fusion.1
  36.2 1.6 reshape.101
  37.7 94.9 %all-to-all-done = bf16[64,5,2048]{2,1,0:T(8,128)(2,1)S(1)} async-done(((bf16[64,5,2048]{2,1,0:T(8,128)(2,1)}), bf16[64,5,2048]{2,1,0:T(8,128)(2,1)S(1)}, u32[]{:S(2)}, u32[]{:S(2)}) %all-to-all-start) | async-done | bytes 1310752 | tf_op jit(solution)/shard_map/all_to_all | solution.py:55
  132.7 1.4 copy-done.2
  134.1 5.8 %all-to-all-start.2 = ((bf16[64,5,2048]{2,1,0:T(8,128)(2,1)}), bf16[64,5,2048]{2,1,0:T(8,128)(2,1)S(1)}, u32[]{:S(2)}, u32[]{:S(2)}) async-start(bf16[64,5,2048]{2,1,0:T(8,128)(2,1)} %reshape.101), calls=%async_computation.2 | async-start | bytes 4194304 | tf_op jit(solution)/shard_map/all_to_all | solution.py:56
  139.9 2.6 reshape.98
  142.5 4.1 fusion.10
  146.6 4.5 multiply_convert_fusion.2
  151.1 3.3 fusion.18
  154.3 1.6 reshape.99
  155.9 83.7 %all-to-all-done.2 = bf16[64,5,2048]{2,1,0:T(8,128)(2,1)S(1)} async-done(((bf16[64,5,2048]{2,1,0:T(8,128)(2,1)}), bf16[64,5,2048]{2,1,0:T(8,128)(2,1)S(1)}, u32[]{:S(2)}, u32[]{:S(2)}) %all-to-all-start.2) | async-done | bytes 1310752 | tf_op jit(solution)/shard_map/all_to_all | solution.py:56
  239.7 1.3 copy-done.1
  241.0 5.8 %all-to-all-start.1 = ((bf16[64,5,2048]{2,1,0:T(8,128)(2,1)}), bf16[64,5,2048]{2,1,0:T(8,128)(2,1)S(1)}, u32[]{:S(2)}, u32[]{:S(2)}) async-start(bf16[64,5,2048]{2,1,0:T(8,128)(2,1)} %reshape.99), calls=%async_computation.1 | async-start | bytes 4194304 | tf_op jit(solution)/shard_map/all_to_all | solution.py:70
  246.8 0.2 reduce-scatter.2.cloned.1.call-start
  247.1 2.6 reshape.102
  249.6 4.5 convolution_convert_fusion
  254.2 3.2 fusion
  257.5 1.3 fusion.4
  258.7 0.6 copy-done.7
  259.3 0.3 copy-done.10
  259.6 1.4 fusion.15
  261.0 1.6 reshape.103
  262.6 83.6 %all-to-all-done.1 = bf16[64,5,2048]{2,1,0:T(8,128)(2,1)S(1)} async-done(((bf16[64,5,2048]{2,1,0:T(8,128)(2,1)}), bf16[64,5,2048]{2,1,0:T(8,128)(2,1)S(1)}, u32[]{:S(2)}, u32[]{:S(2)}) %all-to-all-start.1) | async-done | bytes 1310752 | tf_op jit(solution)/shard_map/all_to_all | solution.py:70
  346.2 6.1 %all-to-all-start.3 = ((bf16[64,5,2048]{2,1,0:T(8,128)(2,1)}), bf16[64,5,2048]{2,1,0:T(8,128)(2,1)}, u32[]{:S(2)}, u32[]{:S(2)}) async-start(bf16[64,5,2048]{2,1,0:T(8,128)(2,1)} %reshape.103), calls=%async_computation.3 | async-start | bytes 4194304 | tf_op jit(solution)/shard_map/all_to_all | solution.py:94
  352.3 0.6 reshape.105
  352.9 2.8 multiply_reduce_fusion
  355.7 0.7 copy.33
  356.3 94.7 %all-to-all-done.3 = bf16[64,5,2048]{2,1,0:T(8,128)(2,1)} async-done(((bf16[64,5,2048]{2,1,0:T(8,128)(2,1)}), bf16[64,5,2048]{2,1,0:T(8,128)(2,1)}, u32[]{:S(2)}, u32[]{:S(2)}) %all-to-all-start.3) | async-done | bytes 1310752 | tf_op jit(solution)/shard_map/all_to_all | solution.py:94
  451.0 2.6 reshape.104
  453.6 1.0 convolution_convert_fusion.3
  (30 shorter events, 0.3 us)
Async XLA Ops:
  7.2 4.3 copy-start
  7.2 135.4 %all-gather.4.cloned.1.call-start = ((), (), s32[]{:S(2)}) async-start(), calls=%async_computation.5 | async-start | bytes 3538944 | tf_op jit(solution)/shard_map/all_gather | solution.py:60
  7.9 138.7 %all-gather.6.cloned.1.call-start = ((), (), s32[]{:S(2)}) async-start(), calls=%async_computation.6 | async-start | bytes 3538944 | tf_op jit(solution)/shard_map/all_gather | solution.py:61
  10.7 0.6 copy-start.4
  13.7 19.4 %copy-start.3 = (bf16[32,2048]{1,0:T(8,128)(2,1)S(1)}, bf16[32,2048]{1,0:T(8,128)(2,1)}, u32[]{:S(2)}) copy-start(bf16[32,2048]{1,0:T(8,128)(2,1)} %param.9) | copy-start | bytes 393220
  13.7 20.2 %copy-start.6 = (f32[32,8]{0,1:T(8,128)S(1)}, f32[32,8]{0,1:T(8,128)}, u32[]{:S(2)}) copy-start(f32[32,8]{0,1:T(8,128)} %param.8) | copy-start | bytes 3076
  13.7 118.9 %all-to-all-start = ((bf16[64,5,2048]{2,1,0:T(8,128)(2,1)}), bf16[64,5,2048]{2,1,0:T(8,128)(2,1)S(1)}, u32[]{:S(2)}, u32[]{:S(2)}) async-start(bf16[64,5,2048]{2,1,0:T(8,128)(2,1)} %reshape.97), calls=%async_computation | async-start | bytes 4194304 | tf_op jit(solution)/shard_map/all_to_all | solution.py:55
  32.4 118.6 %all-gather.8.cloned.1.call-start = ((), (), s32[]{:S(2)}) async-start(), calls=%async_computation.7 | async-start | bytes 3538944 | tf_op jit(solution)/shard_map/all_gather | solution.py:62
  34.0 0.6 copy-start.5
  132.7 1.4 copy-start.2
  134.1 105.6 %all-to-all-start.2 = ((bf16[64,5,2048]{2,1,0:T(8,128)(2,1)}), bf16[64,5,2048]{2,1,0:T(8,128)(2,1)S(1)}, u32[]{:S(2)}, u32[]{:S(2)}) async-start(bf16[64,5,2048]{2,1,0:T(8,128)(2,1)} %reshape.101), calls=%async_computation.2 | async-start | bytes 4194304 | tf_op jit(solution)/shard_map/all_to_all | solution.py:56
  239.7 1.3 copy-start.1
  241.0 105.2 %all-to-all-start.1 = ((bf16[64,5,2048]{2,1,0:T(8,128)(2,1)}), bf16[64,5,2048]{2,1,0:T(8,128)(2,1)S(1)}, u32[]{:S(2)}, u32[]{:S(2)}) async-start(bf16[64,5,2048]{2,1,0:T(8,128)(2,1)} %reshape.99), calls=%async_computation.1 | async-start | bytes 4194304 | tf_op jit(solution)/shard_map/all_to_all | solution.py:70
  246.8 207.7 %reduce-scatter.2.cloned.1.call-start = ((), (), s32[]{:S(2)}) async-start(), calls=%async_computation.8 | async-start | bytes 3538944 | tf_op jit(solution)/shard_map/reduce_scatter | solution.py:83
  254.2 3.2 copy-start.8
  254.2 3.2 copy-start.9
  257.4 1.9 copy-start.7
  257.4 2.1 copy-start.10
  346.2 104.8 %all-to-all-start.3 = ((bf16[64,5,2048]{2,1,0:T(8,128)(2,1)}), bf16[64,5,2048]{2,1,0:T(8,128)(2,1)}, u32[]{:S(2)}, u32[]{:S(2)}) async-start(bf16[64,5,2048]{2,1,0:T(8,128)(2,1)} %reshape.103), calls=%async_computation.3 | async-start | bytes 4194304 | tf_op jit(solution)/shard_map/all_to_all | solution.py:94
Sparse Core Ops, SparseCore 0:
  10.1 38.4 all-gather.3
  50.8 35.3 all-gather.5
  88.3 35.3 all-gather.7
  254.3 41.5 reduce-scatter.1
where the time goes:
time: 462 us; the launch traced here: 461 us
  waiting for transfers between devices  359 us (78%)
  starting transfers between devices  36.8 us (8%)
  matrix products  28 us (6%)
  local copies, waits for them, and re-layouts  21.5 us (5%)
  between operations  14 us (3%)
    all_to_all x1, waiting for transfers between devices, on_device(): lax.all_to_all(send_tokens, 'expert', split_axis=0, concat_axis=0, tiled=...  94.9 us
    all_to_all x1, waiting for transfers between devices, on_device(): lax.all_to_all(row_grad.reshape(n_experts, capacity, model_width), 'exper...  94.7 us
    all_to_all x1, waiting for transfers between devices, on_device(): lax.all_to_all(send_grads, 'expert', split_axis=0, concat_axis=0, tiled=T...  83.7 us
    all_to_all x1, waiting for transfers between devices, on_device(): lax.all_to_all(expert_out.reshape(n_experts, capacity, model_width), 'exp...  83.6 us
    all_to_all x1, starting transfers between devices, on_device(): lax.all_to_all(send_tokens, 'expert', split_axis=0, concat_axis=0, tiled=...  18.7 us
  transfers between devices with their start and end apart: 8, of which 4 were waited for; matrix products, arithmetic and copies ran while one was open for 10% of the time, Pallas kernels for 0%

commit v1 on v0

v1 whole, which is shorter than its diff:
```python
import jax
import jax.numpy as jnp
from jax import lax
from jax.sharding import PartitionSpec as P

NX = 4
TAIL = 128


def contract_last(left, right):
    return lax.dot_general(
        left, right, (((1,), (1,)), ((), ())), preferred_element_type=jnp.float32
    )


def contract_first(left, right):
    return lax.dot_general(
        left, right, (((0,), (0,)), ((), ())), preferred_element_type=jnp.float32
    )


def three_parts(value):
    high = lax.reduce_precision(value, 8, 7)
    rest = value - high
    middle = lax.reduce_precision(rest, 8, 7)
    low = rest - middle
    return [part.astype(jnp.bfloat16) for part in (high, middle, low)]


def tail_of(parts):
    columns = jnp.concatenate(parts, axis=1)
    return jnp.pad(columns, ((0, 0), (0, TAIL - columns.shape[1])))


def on_device(tokens, route_weight, upstream, expert_index, gate_weight, up_weight, down_weight):
    n_experts = lax.axis_size("expert")
    nz = n_experts // NX
    tok_count, top_count = expert_index.shape
    width = tokens.shape[1]
    capacity = max(2, (5 * tok_count * top_count + 4 * n_experts - 1) // (4 * n_experts))
    me = lax.axis_index("expert")
    z_groups = [[z * NX + x for z in range(nz)] for x in range(NX)]
    x_groups = [[z * NX + x for x in range(NX)] for z in range(nz)]

    payload = jnp.concatenate(
        [tokens, upstream,
         tail_of([expert_index.astype(jnp.bfloat16)] + three_parts(route_weight))],
        axis=1,
    )
    full = payload.shape[1]
    gathered = lax.all_gather(payload, "expert", axis=0, tiled=True, axis_index_groups=z_groups)
    w_gate = lax.all_gather(gate_weight, "dp", axis=1, tiled=True)[0]
    w_up = lax.all_gather(up_weight, "dp", axis=1, tiled=True)[0]
    w_down = lax.all_gather(down_weight, "dp", axis=1, tiled=True)[0]

    row_z = me // NX
    named = gathered[:, 2 * width:2 * width + top_count].astype(jnp.float32)
    named = named.reshape(nz, tok_count, top_count)
    experts = (row_z * NX + jnp.arange(NX, dtype=jnp.int32)).astype(jnp.float32)
    match = (named[None] == experts[:, None, None, None]).any(axis=3)
    match_f = match.astype(jnp.bfloat16)
    before = jnp.triu(jnp.ones((tok_count, tok_count), jnp.bfloat16), 1)
    rank = lax.dot_general(
        match_f, before, (((2,), (0,)), ((), ())), preferred_element_type=jnp.float32
    )
    slots = jnp.arange(capacity, dtype=jnp.float32)
    sel = (match[:, :, None, :] & (rank[:, :, None, :] == slots[None, None, :, None])).astype(
        jnp.bfloat16
    )
    rows = lax.dot_general(
        sel.transpose(1, 0, 2, 3).reshape(nz, NX * capacity, tok_count),
        gathered.reshape(nz, tok_count, full),
        (((2,), (1,)), ((0,), (0,))),
        preferred_element_type=jnp.float32,
    ).astype(jnp.bfloat16)
    rows = rows.reshape(nz, NX, capacity, full).transpose(1, 0, 2, 3)
    rows = rows.reshape(NX, nz * capacity, full)
    arrived = lax.all_to_all(
        rows, "expert", split_axis=0, concat_axis=0, tiled=True, axis_index_groups=x_groups
    ).reshape(NX * nz * capacity, full)

    routed_tokens = arrived[:, :width]
    routed_up = arrived[:, width:2 * width]
    tail = arrived[:, 2 * width:].astype(jnp.float32)
    place = tail[:, :top_count] == me.astype(jnp.float32)
    weights = (
        tail[:, top_count:2 * top_count]
        + tail[:, 2 * top_count:3 * top_count]
        + tail[:, 3 * top_count:4 * top_count]
    )
    weight = jnp.sum(jnp.where(place, weights, 0.0), axis=1, keepdims=True)

    gate_value = jnp.dot(routed_tokens, w_gate, preferred_element_type=jnp.float32)
    up_value = jnp.dot(routed_tokens, w_up, preferred_element_type=jnp.float32)
    sig = jax.nn.sigmoid(gate_value)
    activated = gate_value * sig
    slope = sig * (1.0 + gate_value * (1.0 - sig))
    hidden_f = activated * up_value
    hidden = hidden_f.astype(jnp.bfloat16)
    raw_grad = jnp.dot(routed_up, w_down, preferred_element_type=jnp.float32)
    route_value = jnp.sum(hidden.astype(jnp.float32) * raw_grad, axis=1, keepdims=True)
    hidden_grad = raw_grad * weight
    weighted_hidden = (hidden_f * weight).astype(jnp.bfloat16)
    gate_grad = (hidden_grad * up_value * slope).astype(jnp.bfloat16)
    up_grad = (hidden_grad * activated).astype(jnp.bfloat16)
    out_rows = contract_last(weighted_hidden, w_down).astype(jnp.bfloat16)
    row_grad = (contract_last(gate_grad, w_gate) + contract_last(up_grad, w_up)).astype(
        jnp.bfloat16
    )
    route_tail = tail_of(three_parts(jnp.where(place, route_value, 0.0)))
    back = jnp.concatenate([out_rows, row_grad, route_tail], axis=1)
    returned = lax.all_to_all(
        back.reshape(NX, nz * capacity, full),
        "expert", split_axis=0, concat_axis=0, tiled=True, axis_index_groups=x_groups,
    )
    down_grad = lax.psum_scatter(
        contract_first(routed_up, weighted_hidden).astype(jnp.bfloat16),
        "dp", scatter_dimension=0, tiled=True,
    )[None]
    returned = returned.reshape(NX, nz, capacity, full).transpose(1, 0, 2, 3)
    partial = lax.dot_general(
        sel.transpose(1, 3, 0, 2).reshape(nz, tok_count, NX * capacity),
        returned.reshape(nz, NX * capacity, full),
        (((2,), (1,)), ((0,), (0,))),
        preferred_element_type=jnp.float32,
    ).astype(jnp.bfloat16)
    summed = lax.psum_scatter(
        partial.reshape(nz * tok_count, full), "expert", scatter_dimension=0, tiled=True,
        axis_index_groups=z_groups,
    )
    combined = summed[:, :width]
    token_grad = summed[:, width:2 * width]
    last = summed[:, 2 * width:].astype(jnp.float32)
    route_grad = (
        last[:, :top_count] + last[:, top_count:2 * top_count] + last[:, 2 * top_count:3 * top_count]
    )
    return (combined, token_grad, route_grad, down_grad)


def solution(mesh):
    return jax.shard_map(
        on_device,
        mesh=mesh,
        in_specs=(
            P(("dp", "expert"), None),
            P(("dp", "expert"), None),
            P(("dp", "expert"), None),
            P(("dp", "expert"), None),
            P("expert", "dp", None),
            P("expert", "dp", None),
            P("expert", "dp", None),
        ),
        out_specs=(
            P(("dp", "expert"), None),
            P(("dp", "expert"), None),
            P(("dp", "expert"), None),
            P("expert", "dp", None),
        ),
        check_vma=False,
    )
```

time: 462 us -> 391 us (0.85)
  waiting for transfers between devices: 359 us -> 315 us
  starting transfers between devices: 36.8 us -> 8.76 us
  local copies, waits for them, and re-layouts: 21.5 us -> 11.6 us
    all_to_all x4 -> x2, waiting for transfers between devices: 357 us -> 57 us  [the longest x1 33.1 us: on_device(): lax.all_to_all(back.reshape(NX, nz * capacity, full), 'expert', split_axi...]
    all_gather x3 -> x4, waiting for transfers between devices: 0.02 us -> 143 us  [the longest x1 80.4 us: on_device(): lax.all_gather(payload, 'expert', axis=0, tiled=True, axis_index_groups=z...]
    unnamed x4 -> x7, waiting for transfers between devices: 2.07 us -> 77.2 us
    reduce_scatter x1, waiting for transfers between devices: 0.01 us -> 38.1 us  [on_device(): lax.psum_scatter(contract_first(routed_up, weighted_hidden).astype(jnp.bf...]
    all_to_all x4 -> x2, starting transfers between devices: 36.5 us -> 8.56 us  [the longest x1 4.31 us: on_device(): lax.all_to_all(rows, 'expert', split_axis=0, concat_axis=0, tiled=True, a...]
    reshape x9 -> x1, local copies, waits for them, and re-layouts: 14.9 us -> 1.8 us  [on_device(): rows = rows.reshape(NX, nz * capacity, full)]
    dot_general x3 -> x4, matrix products: 5.3 us -> 11.6 us  [the longest x1 4.8 us: on_device(): raw_grad = jnp.dot(routed_up, w_down, preferred_element_type=jnp.float32)]
    dot_general x3 -> x1, matrix products: 8.3 us -> 3.51 us  [contract_first(): lax.dot_general(left, right, (((0,), (0,)), ((), ())), preferred_element_...]
  transfers between devices with their start and end apart: 8 -> 8, of which waited for: 4 -> 7; matrix products, arithmetic and copies ran while one was open for 10% -> 6% of each run, Pallas kernels for 0% -> 0%
where the time goes in v1:
time: 391 us; the launch traced here: 386 us
  waiting for transfers between devices  315 us (81%)
  matrix products  30.6 us (8%)
  between operations  14.3 us (4%)
  local copies, waits for them, and re-layouts  11.6 us (3%)
  starting transfers between devices  8.76 us (2%)
  other arithmetic  5.88 us (2%)
    all_gather x1, waiting for transfers between devices, on_device(): lax.all_gather(payload, 'expert', axis=0, tiled=True, axis_index_groups=z...  80.4 us
    unnamed x7, waiting for transfers between devices  77.2 us
    reduce_scatter x1, waiting for transfers between devices, on_device(): lax.psum_scatter(contract_first(routed_up, weighted_hidden).astype(jnp.bf...  38.1 us
    all_gather x1, waiting for transfers between devices, on_device(): w_up = lax.all_gather(up_weight, 'dp', axis=1, tiled=True)[0]  33.4 us
    all_to_all x1, waiting for transfers between devices, on_device(): lax.all_to_all(back.reshape(NX, nz * capacity, full), 'expert', split_axi...  33.1 us
    all_gather x1, waiting for transfers between devices, on_device(): w_gate = lax.all_gather(gate_weight, 'dp', axis=1, tiled=True)[0]  29.3 us
    all_to_all x1, waiting for transfers between devices, on_device(): lax.all_to_all(rows, 'expert', split_axis=0, concat_axis=0, tiled=True, a...  23.9 us
  transfers between devices with their start and end apart: 8, of which 7 were waited for; matrix products, arithmetic and copies ran while one was open for 6% of the time, Pallas kernels for 0%

profile of v1, /device:TPU:24, one launch (start us, length us, event | category | flops | bytes accessed | tf_op | source)
XLA Modules:
  0.0 386.4 jit_solution(6851570231931170417)
XLA Ops:
  7.2 0.7 convert_element_type.74
  7.9 0.7 reduce-precision_convert_fusion.3
  8.6 0.1 copy.67
  8.7 1.7 fusion.33
  10.5 0.7 all-gather.11.cloned.1.call-update
  11.2 0.7 all-gather.7.cloned.1.call-update
  11.9 0.5 all-gather.9.cloned.1.call-update
  12.6 80.4 %all-gather.5.cloned.1.call-done = bf16[512,4224]{1,0:T(8,128)(2,1)} async-done(((bf16[32,4224]{1,0:T(8,128)(2,1)}), bf16[512,4224]{1,0:T(8,128)(2,1)}) %all-gather.5.cloned.1.call-update) | async-done | bytes 4325392 | tf_op jit(solution)/shard_map/all_gather | solution.py:51
  93.0 0.9 slice.56
  93.9 0.1 copy.47
  94.0 0.2 compare_reduce_fusion
  94.2 0.1 fusion.43
  94.3 0.1 fusion.37
  94.4 3.2 convolution_convert_fusion.1
  97.6 0.3 copy.49
  97.9 1.0 copy.50
  99.0 1.8 copy.51
  100.8 4.3 %all-to-all-start = ((bf16[4,80,4224]{2,1,0:T(8,128)(2,1)}), bf16[4,80,4224]{2,1,0:T(8,128)(2,1)S(1)}, u32[]{:S(2)}, u32[]{:S(2)}) async-start(bf16[4,80,4224]{2,1,0:T(8,128)(2,1)} %copy.51), calls=%async_computation | async-start | bytes 5406720 | tf_op jit(solution)/shard_map/all_to_all | solution.py:78
  105.1 23.9 %all-to-all-done = bf16[4,80,4224]{2,1,0:T(8,128)(2,1)S(1)} async-done(((bf16[4,80,4224]{2,1,0:T(8,128)(2,1)}), bf16[4,80,4224]{2,1,0:T(8,128)(2,1)S(1)}, u32[]{:S(2)}, u32[]{:S(2)}) %all-to-all-start) | async-done | bytes 2703392 | tf_op jit(solution)/shard_map/all_to_all | solution.py:78
  129.0 0.1 copy.63
  129.2 4.8 %fusion.2 = f32[320,768]{1,0:T(8,128)} fusion(bf16[1,2048,768]{2,1,0:T(8,128)(2,1)} %all-gather.11.cloned.1.call-done, bf16[320,4224]{1,0:T(8,128)(2,1)S(1)} %bitcast.70), kind=kOutput, calls=%fused_computation.6 | convolution fusion | flops 1006632960 | bytes 5439488 | tf_op jit(solution)/shard_map/dot_general | solution.py:100
  134.0 29.3 %all-gather.7.cloned.1.call-done = bf16[1,2048,768]{2,1,0:T(8,128)(2,1)} async-done(((bf16[1,256,768]{2,1,0:T(8,128)(2,1)}), bf16[1,2048,768]{2,1,0:T(8,128)(2,1)}) %all-gather.7.cloned.1.call-update) | async-done | bytes 3145744 | tf_op jit(solution)/shard_map/all_gather | solution.py:52
  163.3 4.0 %fusion.12 = f32[320,768]{1,0:T(8,128)} fusion(bf16[1,2048,768]{2,1,0:T(8,128)(2,1)} %all-gather.7.cloned.1.call-done, bf16[320,4224]{1,0:T(8,128)(2,1)S(1)} %bitcast.71), kind=kOutput, calls=%fused_computation.16 | convolution fusion | flops 1006632960 | bytes 5439488 | tf_op jit(solution)/shard_map/dot_general | solution.py:93
  167.3 33.4 %all-gather.9.cloned.1.call-done = bf16[1,2048,768]{2,1,0:T(8,128)(2,1)} async-done(((bf16[1,256,768]{2,1,0:T(8,128)(2,1)}), bf16[1,2048,768]{2,1,0:T(8,128)(2,1)}) %all-gather.9.cloned.1.call-update) | async-done | bytes 3145744 | tf_op jit(solution)/shard_map/all_gather | solution.py:53
  200.7 4.8 %multiply_convert_fusion.2 = (bf16[320,768]{1,0:T(8,128)(2,1)S(1)}, f32[320]{0:T(512)S(1)}, f32[320,768]{1,0:T(8,128)}) fusion(f32[320]{0:T(512)S(1)} %get-tuple-element.20, f32[320,768]{1,0:T(8,128)} %fusion.12, f32[320,768]{1,0:T(8,128)} %fusion.2, bf16[1,2048,768]{2,1,0:T(8,128)(2,1)} %all-gather.9.cloned.1.call-done, bf16[320,4224]{1,0:T(8,128)(2,1)S(1)} %bitcast.72), kind=kOutput, calls=%fused_computation.29 | convolution fusion | flops 1009336000 | bytes 7900416 | tf_op jit(solution)/shard_map/dot_general | solution.py:94
  205.4 0.1 copy.53
  205.6 4.0 %fusion.6 = f32[320,2048]{1,0:T(8,128)S(1)} fusion(bf16[1,2048,768]{2,1,0:T(8,128)(2,1)} %all-gather.9.cloned.1.call-done, f32[320,768]{1,0:T(8,128)} %fusion.2, f32[320]{0:T(512)S(1)} %get-tuple-element.20, f32[320,768]{1,0:T(8,128)} %fusion.12), kind=kOutput, calls=%fused_computation.10 | convolution fusion | flops 1008353280 | bytes 7734528 | tf_op jit(solution)/shard_map/dot_general | solution.py:11
  209.6 1.2 fusion.21
  210.9 0.6 copy-done.3
  211.5 0.3 copy-done.4
  211.8 0.3 copy-done.5
  212.0 0.3 copy-done.6
  212.3 1.5 fusion.18
  213.9 1.7 fusion.17
  215.6 4.3 %all-to-all-start.1 = ((bf16[4,80,4224]{2,1,0:T(8,128)(2,1)}), bf16[4,80,4224]{2,1,0:T(8,128)(2,1)S(1)}, u32[]{:S(2)}, u32[]{:S(2)}) async-start(bf16[4,80,4224]{2,1,0:T(8,128)(2,1)} %bitcast.64), calls=%async_computation.1 | async-start | bytes 5406720 | tf_op jit(solution)/shard_map/all_to_all | solution.py:112
  219.8 0.1 fusion.36
  220.0 33.1 %all-to-all-done.1 = bf16[4,80,4224]{2,1,0:T(8,128)(2,1)S(1)} async-done(((bf16[4,80,4224]{2,1,0:T(8,128)(2,1)}), bf16[4,80,4224]{2,1,0:T(8,128)(2,1)S(1)}, u32[]{:S(2)}, u32[]{:S(2)}) %all-to-all-start.1) | async-done | bytes 2703392 | tf_op jit(solution)/shard_map/all_to_all | solution.py:112
  253.1 1.0 copy.54
  254.1 0.3 copy.55
  254.4 3.5 convolution_convert_fusion
  257.9 1.7 copy-done.1
  259.6 3.5 convolution_convert_fusion.2
  263.2 75.3 %reduce-scatter.7.cloned.1.call-done = bf16[32,4224]{1,0:T(8,128)(2,1)} async-done(((bf16[512,4224]{1,0:T(8,128)(2,1)}), bf16[32,4224]{1,0:T(8,128)(2,1)}) %reduce-scatter.7.cloned.1.call-update) | async-done | bytes 270352
  338.4 0.7 slice.66
  339.1 0.1 copy.66
  339.2 0.6 slice_add_fusion.2
  339.9 1.7 fusion.52
  341.5 38.1 %reduce-scatter.5.cloned.1.call-done = bf16[256,768]{1,0:T(8,128)(2,1)} async-done(((bf16[2048,768]{1,0:T(8,128)(2,1)}), bf16[256,768]{1,0:T(8,128)(2,1)}) %reduce-scatter.5.cloned.1.call-update) | async-done | bytes 393232 | tf_op jit(solution)/shard_map/reduce_scatter | solution.py:116
  (29 shorter events, 0.5 us)
Async XLA Ops:
  7.2 85.8 %all-gather.5.cloned.1.call-start = ((), (), s32[]{:S(2)}) async-start(), calls=%async_computation.4 | async-start | bytes 4595712 | tf_op jit(solution)/shard_map/all_gather | solution.py:51
  10.4 118.7 %all-gather.11.cloned.1.call-start = ((), (), s32[]{:S(2)}) async-start(), calls=%async_computation.7 | async-start | bytes 3538944 | tf_op jit(solution)/shard_map/all_gather | solution.py:54
  11.2 152.1 %all-gather.7.cloned.1.call-start = ((), (), s32[]{:S(2)}) async-start(), calls=%async_computation.5 | async-start | bytes 3538944 | tf_op jit(solution)/shard_map/all_gather | solution.py:52
  11.9 188.8 %all-gather.9.cloned.1.call-start = ((), (), s32[]{:S(2)}) async-start(), calls=%async_computation.6 | async-start | bytes 3538944 | tf_op jit(solution)/shard_map/all_gather | solution.py:53
  100.8 28.2 %all-to-all-start = ((bf16[4,80,4224]{2,1,0:T(8,128)(2,1)}), bf16[4,80,4224]{2,1,0:T(8,128)(2,1)S(1)}, u32[]{:S(2)}, u32[]{:S(2)}) async-start(bf16[4,80,4224]{2,1,0:T(8,128)(2,1)} %copy.51), calls=%async_computation | async-start | bytes 5406720 | tf_op jit(solution)/shard_map/all_to_all | solution.py:78
  128.9 71.7 %copy-start = (bf16[4,80,4224]{2,1,0:T(8,128)(2,1)}, bf16[4,80,4224]{2,1,0:T(8,128)(2,1)S(1)}, u32[]{:S(2)}) copy-start(bf16[4,80,4224]{2,1,0:T(8,128)(2,1)S(1)} %all-to-all-done) | copy-start | bytes 8110084
  205.6 4.0 %copy-start.2 = (bf16[1,2048,768]{2,1,0:T(8,128)(2,1)S(1)}, bf16[1,2048,768]{2,1,0:T(8,128)(2,1)}, u32[]{:S(2)}) copy-start(bf16[1,2048,768]{2,1,0:T(8,128)(2,1)} %all-gather.11.cloned.1.call-done) | copy-start | bytes 9437188
  209.6 1.9 copy-start.3
  209.6 2.1 copy-start.4
  209.6 2.4 copy-start.5
  209.6 2.7 copy-start.6
  215.6 37.5 %all-to-all-start.1 = ((bf16[4,80,4224]{2,1,0:T(8,128)(2,1)}), bf16[4,80,4224]{2,1,0:T(8,128)(2,1)S(1)}, u32[]{:S(2)}, u32[]{:S(2)}) async-start(bf16[4,80,4224]{2,1,0:T(8,128)(2,1)} %bitcast.64), calls=%async_computation.1 | async-start | bytes 5406720 | tf_op jit(solution)/shard_map/all_to_all | solution.py:112
  219.8 118.6 %reduce-scatter.7.cloned.1.call-start = ((), (), s32[]{:S(2)}) async-start(), calls=%async_computation.9 | async-start | bytes 4595712
  257.9 1.8 copy-start.1
  257.9 121.7 %reduce-scatter.5.cloned.1.call-start = ((), (), s32[]{:S(2)}) async-start(), calls=%async_computation.8 | async-start | bytes 3538944 | tf_op jit(solution)/shard_map/reduce_scatter | solution.py:116
Sparse Core Ops, SparseCore 0:
  10.6 82.2 all-gather.4
  95.1 30.5 all-gather.10
  127.9 35.3 all-gather.6
  165.2 35.3 all-gather.8
  258.0 80.3 reduce-scatter.6
  341.7 37.8 reduce-scatter.4

commit v2 on v1

--- a/solution.py
+++ b/solution.py
@@ -1,10 +1,223 @@
+import functools
 import jax
 import jax.numpy as jnp
 from jax import lax
+from jax.experimental import pallas as pl
+from jax.experimental.pallas import tpu as pltpu
 from jax.sharding import PartitionSpec as P
 
 NX = 4
+NC = 2
 TAIL = 128
+
+
+MESH = pl.DeviceIdType.MESH
+
+
+def ring_ends(nz):
+    me = lax.axis_index("expert")
+    z, x = me // NX, me % NX
+    right = lax.rem(z + 1, nz) * NX + x
+    left = lax.rem(z + nz - 1, nz) * NX + x
+    return z, ({"expert": right}, {"expert": left})
+
+
+def greet(others):
+    barrier = pltpu.get_barrier_semaphore()
+    for other in others:
+        pl.semaphore_signal(barrier, inc=1, device_id=other, device_id_type=MESH)
+    pl.semaphore_wait(barrier, len(others))
+
+
+def gather_kernel(
+    nz, ny, own_ref, w0_ref, w1_ref, w2_ref, out_ref, g0_ref, g1_ref, g2_ref,
+    local_sem, send_sem, recv_sem, wsend_sem, wrecv_sem,
+):
+    z, ends = ring_ends(nz)
+    dp = lax.axis_index("dp")
+    y, core = dp // NC, dp % NC
+    behind = (lax.rem(y + ny - 1, ny) * NC + core, lax.rem(y + 1, ny) * NC + core)
+    across = lax.rem(y + 2, ny) * NC + core
+    ahead = ({"dp": behind[1]}, {"dp": behind[0]})
+    sibling = {"dp": y * NC + 1 - core}
+    greet(ends + ahead + (sibling,))
+    half = nz // 2
+    rows = own_ref.shape[0] // 2
+    owned = (w0_ref, w1_ref, w2_ref)
+    filled = (g0_ref, g1_ref, g2_ref)
+    wrows = w0_ref.shape[0]
+
+    def weight(j, k):
+        own, full = owned[j], filled[j]
+        if k < 2:
+            source, target, to = own, full.at[dp], ahead[k]
+        elif k < 4:
+            part = pl.ds((k - 2) * (wrows // 2), wrows // 2)
+            source = target = full.at[behind[k - 2], part]
+            to = ahead[k - 2]
+        elif k == 4:
+            source, target, to = own, full.at[dp], sibling
+        elif k < 7:
+            source = target = full.at[behind[k - 5]]
+            to = sibling
+        else:
+            part = pl.ds((k - 7) * (wrows // 2), wrows // 2)
+            source = target = full.at[across, part]
+            to = sibling
+        return pltpu.make_async_remote_copy(
+            src_ref=source, dst_ref=target,
+            send_sem=wsend_sem.at[j, k], recv_sem=wrecv_sem.at[j, k],
+            device_id=to, device_id_type=MESH,
+        )
+
+    def copy(step, way, chunk):
+        block = lax.rem(z - step + nz, nz) if way == 0 else lax.rem(z + step, nz)
+        part = pl.ds(chunk * rows, rows)
+        source = own_ref.at[part] if step == 0 else out_ref.at[block, part]
+        return pltpu.make_async_remote_copy(
+            src_ref=source,
+            dst_ref=out_ref.at[block, part],
+            send_sem=send_sem.at[step, way, chunk],
+            recv_sem=recv_sem.at[step, way, chunk],
+            device_id=ends[way], device_id_type=MESH,
+        )
+
+    keep = [pltpu.make_async_copy(own_ref, out_ref.at[z], local_sem.at[3])] + [
+        pltpu.make_async_copy(owned[j], filled[j].at[dp], local_sem.at[j]) for j in range(3)
+    ]
+    lanes = [(way, chunk) for chunk in range(2) for way in range(2)]
+    for step in range(half):
+        for way, chunk in lanes:
+            if step > 0:
+                copy(step - 1, way, chunk).wait_recv()
+            if step < half - 1 or chunk == way:
+                copy(step, way, chunk).start()
+        if step == 0:
+            for j in range(3):
+                for k in (0, 1):
+                    weight(j, k).start()
+            for j in range(3):
+                weight(j, 4).start()
+            for one in keep:
+                one.start()
+        j = {2: 0, 4: 1, 5: 2}.get(step)
+        if j is not None:
+            for k in range(2):
+                weight(j, k).wait_recv()
+                weight(j, 2 + k).start()
+                weight(j, 5 + k).start()
+        if step == half - 1:
+            for j in range(2):
+                for k in range(2):
+                    weight(j, 2 + k).wait_recv()
+                    weight(j, 7 + k).start()
+    for way in range(2):
+        copy(half - 1, way, way).wait_recv()
+    for k in range(2):
+        weight(2, 2 + k).wait_recv()
+        weight(2, 7 + k).start()
+    for j in range(3):
+        for k in range(4, 9):
+            weight(j, k).wait_recv()
+    for j in range(3):
+        for k in range(9):
+            weight(j, k).wait_send()
+    for step in range(half):
+        for way, chunk in lanes:
+            if step < half - 1 or chunk == way:
+                copy(step, way, chunk).wait_send()
+    for one in keep:
+        one.wait()
+
+
+def ring_gather(payload, weights, nz, ny):
+    rows, full = payload.shape
+    half = nz // 2
+    shards = [jax.ShapeDtypeStruct((ny * NC,) + w.shape, w.dtype) for w in weights]
+    return pl.pallas_call(
+        functools.partial(gather_kernel, nz, ny),
+        out_shape=[jax.ShapeDtypeStruct((nz, rows, full), payload.dtype)] + shards,
+        in_specs=[pl.BlockSpec(memory_space=pltpu.VMEM)] * 4,
+        out_specs=[pl.BlockSpec(memory_space=pl.ANY)] * 4,
+        scratch_shapes=[
+            pltpu.SemaphoreType.DMA((4,)),
+            pltpu.SemaphoreType.DMA((half, 2, 2)),
+            pltpu.SemaphoreType.DMA((half, 2, 2)),
+            pltpu.SemaphoreType.DMA((3, 9)),
+            pltpu.SemaphoreType.DMA((3, 9)),
+        ],
+        compiler_params=pltpu.CompilerParams(collective_id=0, has_side_effects=True),
+    )(payload, *weights)
+
+
+def reduce_kernel(nz, part_ref, out_ref, held, going, send_sem, recv_sem):
+    z, ends = ring_ends(nz)
+    greet(ends)
+    half = nz // 2
+    rows = out_ref.shape[0] // 2
+
+    def copy(step, way, chunk):
+        return pltpu.make_async_remote_copy(
+            src_ref=going.at[step, way, chunk],
+            dst_ref=held.at[step, way, chunk],
+            send_sem=send_sem.at[step, way, chunk],
+            recv_sem=recv_sem.at[step, way, chunk],
+            device_id=ends[way],
+            device_id_type=pl.DeviceIdType.MESH,
+        )
+
+    def first(way, chunk):
+        return 0 if chunk == way else 1
+
+    lanes = [(way, chunk) for chunk in range(2) for way in range(2)]
+    for step in range(half):
+        for way, chunk in sorted(lanes, key=lambda lane: lane[0] != lane[1]):
+            start = first(way, chunk)
+            if step < start:
+                continue
+            distance = half - step
+            block = lax.rem(z + distance, nz) if way == 0 else lax.rem(z - distance + nz, nz)
+            value = part_ref[block, pl.ds(chunk * rows, rows), :]
+            if step > start:
+                copy(step - 1, way, chunk).wait_recv()
+                value = (
+                    value.astype(jnp.float32)
+                    + held[step - 1, way, chunk].astype(jnp.float32)
+                ).astype(value.dtype)
+            going[step, way, chunk] = value
+            copy(step, way, chunk).start()
+    for chunk in range(2):
+        total = part_ref[z, pl.ds(chunk * rows, rows), :].astype(jnp.float32)
+        for way in range(2):
+            copy(half - 1, way, chunk).wait_recv()
+            total = total + held[half - 1, way, chunk].astype(jnp.float32)
+        out_ref[pl.ds(chunk * rows, rows), :] = total.astype(out_ref.dtype)
+    for step in range(half):
+        for way, chunk in lanes:
+            if step >= first(way, chunk):
+                copy(step, way, chunk).wait_send()
+
+
+def ring_reduce(partial):
+    nz, rows, full = partial.shape
+    half = nz // 2
+    slots = (half, 2, 2, rows // 2, full)
+    return pl.pallas_call(
+        functools.partial(reduce_kernel, nz),
+        out_shape=jax.ShapeDtypeStruct((rows, full), partial.dtype),
+        in_specs=[pl.BlockSpec(memory_space=pltpu.VMEM)],
+        out_specs=pl.BlockSpec(memory_space=pltpu.VMEM),
+        scratch_shapes=[
+            pltpu.VMEM(slots, partial.dtype),
+            pltpu.VMEM(slots, partial.dtype),
+            pltpu.SemaphoreType.DMA((half, 2, 2)),
+            pltpu.SemaphoreType.DMA((half, 2, 2)),
+        ],
+        compiler_params=pltpu.CompilerParams(collective_id=1, has_side_effects=True),
+        cost_estimate=pl.CostEstimate(
+            flops=0, bytes_accessed=100_000_000, transcendentals=0
+        ),
+    )(partial)
 
 
 def contract_last(left, right):
@@ -39,23 +252,22 @@
     width = tokens.shape[1]
     capacity = max(2, (5 * tok_count * top_count + 4 * n_experts - 1) // (4 * n_experts))
     me = lax.axis_index("expert")
-    z_groups = [[z * NX + x for z in range(nz)] for x in range(NX)]
+    n_dp = lax.axis_size("dp")
+    ny = n_dp // NC
     x_groups = [[z * NX + x for x in range(NX)] for z in range(nz)]
-
     payload = jnp.concatenate(
         [tokens, upstream,
          tail_of([expert_index.astype(jnp.bfloat16)] + three_parts(route_weight))],
         axis=1,
     )
     full = payload.shape[1]
-    gathered = lax.all_gather(payload, "expert", axis=0, tiled=True, axis_index_groups=z_groups)
-    w_gate = lax.all_gather(gate_weight, "dp", axis=1, tiled=True)[0]
-    w_up = lax.all_gather(up_weight, "dp", axis=1, tiled=True)[0]
-    w_down = lax.all_gather(down_weight, "dp", axis=1, tiled=True)[0]
+    gathered, *shards = ring_gather(
+        payload, (gate_weight[0], up_weight[0], down_weight[0]), nz, ny
+    )
+    w_gate, w_up, w_down = (one.reshape(width, -1) for one in shards)
 
     row_z = me // NX
-    named = gathered[:, 2 * width:2 * width + top_count].astype(jnp.float32)
-    named = named.reshape(nz, tok_count, top_count)
+    named = gathered[:, :, 2 * width:2 * width + top_count].astype(jnp.float32)
     experts = (row_z * NX + jnp.arange(NX, dtype=jnp.int32)).astype(jnp.float32)
     match = (named[None] == experts[:, None, None, None]).any(axis=3)
     match_f = match.astype(jnp.bfloat16)
@@ -69,7 +281,7 @@
     )
     rows = lax.dot_general(
         sel.transpose(1, 0, 2, 3).reshape(nz, NX * capacity, tok_count),
-        gathered.reshape(nz, tok_count, full),
+        gathered,
         (((2,), (1,)), ((0,), (0,))),
         preferred_element_type=jnp.float32,
     ).astype(jnp.bfloat16)
@@ -124,10 +336,7 @@
         (((2,), (1,)), ((0,), (0,))),
         preferred_element_type=jnp.float32,
     ).astype(jnp.bfloat16)
-    summed = lax.psum_scatter(
-        partial.reshape(nz * tok_count, full), "expert", scatter_dimension=0, tiled=True,
-        axis_index_groups=z_groups,
-    )
+    summed = ring_reduce(partial)
     combined = summed[:, :width]
     token_grad = summed[:, width:2 * width]
     last = summed[:, 2 * width:].astype(jnp.float32)

time: 391 us -> 246 us (0.63)
  waiting for transfers between devices: 315 us -> 65.5 us
  Pallas kernels: 0 us -> 116 us
  matrix products: 30.6 us -> 23.4 us
    all_gather x4 -> x0, waiting for transfers between devices: 143 us -> none  [the longest x1 80.4 us: on_device(): lax.all_gather(payload, 'expert', axis=0, tiled=True, axis_index_groups=z...]
    pallas_call x0 -> x2, Pallas kernels: none -> 116 us  [the longest x1 62.2 us: ring_gather(): pl.pallas_call(functools.partial(gather_kernel, nz, ny), out_shape=[jax.S...]
    unnamed x7 -> x1, waiting for transfers between devices: 77.2 us -> 0.02 us
    reduce_scatter x1, waiting for transfers between devices: 38.1 us -> 0.01 us  [on_device(): lax.psum_scatter(contract_first(routed_up, weighted_hidden).astype(jnp.bf...]
    all_to_all x1, waiting for transfers between devices: 23.9 us -> 33.4 us  [on_device(): lax.all_to_all(rows, 'expert', split_axis=0, concat_axis=0, tiled=True, a...]
  transfers between devices with their start and end apart: 8 -> 3, of which waited for: 7 -> 2; matrix products, arithmetic and copies ran while one was open for 6% -> 7% of each run, Pallas kernels for 0% -> 22%
where the time goes in v2:
time: 246 us; the launch traced here: 245 us
  Pallas kernels  116 us (47%)
  waiting for transfers between devices  65.5 us (27%)
  matrix products  23.4 us (10%)
  between operations  14.3 us (6%)
  local copies, waits for them, and re-layouts  10 us (4%)
  starting transfers between devices  8.24 us (3%)
  other arithmetic  7.07 us (3%)
    pallas_call x1, Pallas kernels, ring_gather(): pl.pallas_call(functools.partial(gather_kernel, nz, ny), out_shape=[jax.S...  62.2 us
    pallas_call x1, Pallas kernels, ring_reduce(): pl.pallas_call(functools.partial(reduce_kernel, nz), out_shape=jax.ShapeD...  53.8 us
    all_to_all x1, waiting for transfers between devices, on_device(): lax.all_to_all(rows, 'expert', split_axis=0, concat_axis=0, tiled=True, a...  33.4 us
    all_to_all x1, waiting for transfers between devices, on_device(): lax.all_to_all(back.reshape(NX, nz * capacity, full), 'expert', split_axi...  32.1 us
    dot_general x3, matrix products, contract_last(): lax.dot_general(left, right, (((1,), (1,)), ((), ())), preferred_element_...  6.26 us
  transfers between devices with their start and end apart: 3, of which 2 were waited for; matrix products, arithmetic and copies ran while one was open for 7% of the time, Pallas kernels for 22%

profile of v2, /device:TPU:24, one launch (start us, length us, event | category | flops | bytes accessed | tf_op | source)
XLA Modules:
  0.0 244.5 jit_solution(13312134355721602091)
XLA Ops:
  7.2 0.7 reduce_precision.12
  7.9 0.8 copy.62
  8.6 0.7 convert_element_type.76
  9.3 0.1 eq.65
  9.4 0.1 copy.64
  9.5 0.1 copy.61
  9.6 0.1 fusion.34
  9.7 1.7 pad_maximum_fusion.own_ref
  11.4 62.2 %shard_map.102 = (bf16[16,32,4224]{2,1,0:T(8,128)(2,1)}, bf16[8,256,768]{2,1,0:T(8,128)(2,1)}, bf16[8,256,768]{2,1,0:T(8,128)(2,1)}, bf16[8,256,768]{2,1,0:T(8,128)(2,1)}) custom-call(bf16[32,4224]{1,0:T(8,128)(2,1)} %pad_maximum_fusion.own_ref, bf16[256,768]{1,0:T(8,128)(2,1)} %bitcast.56, bf16[256,768]{1,0:T(8,128)(2,1)} %bitcast.57, bf16[256,768]{1,0:T(8,128)(2,1)} %bitcast.58), custom_call_target="tpu_custom_call" | custom-call | tf_op jit(solution)/shard_map/pallas_call | solution.py:137
  73.5 0.9 slice_convert_fusion
  74.5 0.1 copy.65
  74.6 0.2 compare_reduce_fusion
  74.8 0.1 fusion.30
  74.9 0.1 fusion.19
  75.0 3.2 %convolution_convert_fusion.1 = bf16[16,20,4224]{2,1,0:T(8,128)(2,1)S(1)} fusion(bf16[16,32,4224]{2,1,0:T(8,128)(2,1)} %get-tuple-element.8, pred[16,20,32]{2,0,1:T(8,128)(4,1)S(1)} %fusion.19), kind=kOutput, calls=%fused_computation.1 | convolution fusion | flops 87859200 | bytes 7038976 | tf_op jit(solution)/shard_map/dot_general | solution.py:282
  78.3 0.3 copy.67
  78.5 1.0 copy.68
  79.6 1.8 copy.69
  81.4 4.3 %all-to-all-start = ((bf16[4,80,4224]{2,1,0:T(8,128)(2,1)}), bf16[4,80,4224]{2,1,0:T(8,128)(2,1)S(1)}, u32[]{:S(2)}, u32[]{:S(2)}) async-start(bf16[4,80,4224]{2,1,0:T(8,128)(2,1)} %copy.69), calls=%async_computation | async-start | bytes 5406720 | tf_op jit(solution)/shard_map/all_to_all | solution.py:290
  85.7 0.0 reduce-scatter.2.cloned.1.call-start
  85.7 33.4 %all-to-all-done = bf16[4,80,4224]{2,1,0:T(8,128)(2,1)S(1)} async-done(((bf16[4,80,4224]{2,1,0:T(8,128)(2,1)}), bf16[4,80,4224]{2,1,0:T(8,128)(2,1)S(1)}, u32[]{:S(2)}, u32[]{:S(2)}) %all-to-all-start) | async-done | bytes 2703392 | tf_op jit(solution)/shard_map/all_to_all | solution.py:290
  119.1 0.1 copy.77
  119.3 3.2 %fusion.5 = f32[320,768]{1,0:T(8,128)S(1)} fusion(bf16[2048,768]{1,0:T(8,128)(2,1)} %bitcast.67, bf16[320,4224]{1,0:T(8,128)(2,1)S(1)} %bitcast.52), kind=kOutput, calls=%fused_computation.11 | convolution fusion | flops 1006632960 | bytes 5439488 | tf_op jit(solution)/shard_map/dot_general | solution.py:312
  122.5 1.2 fusion.9
  123.8 0.0 copy-done.4
  123.8 1.1 copy-done
  124.9 2.3 multiply_convert_fusion.2
  127.2 3.6 %convolution_convert_fusion.2 = bf16[2048,768]{1,0:T(8,128)(2,1)} fusion(bf16[320,768]{1,0:T(8,128)(2,1)S(1)} %get-tuple-element.34, bf16[320,4224]{1,0:T(8,128)(2,1)S(1)} %bitcast.55), kind=kOutput, calls=%fused_computation.4 | convolution fusion | flops 1008205824 | bytes 4947968 | tf_op jit(solution)/shard_map/dot_general | solution.py:230
  130.8 0.0 reduce-scatter.2.cloned.1.call-update
  130.9 0.1 copy.71
  131.0 3.3 %convolution_convert_fusion.3 = bf16[320,2048]{1,0:T(8,128)(2,1)S(1)} fusion(bf16[320,768]{1,0:T(8,128)(2,1)S(1)} %get-tuple-element.34, bf16[2048,768]{1,0:T(8,128)(2,1)} %bitcast.68), kind=kOutput, calls=%fused_computation.9 | convolution fusion | flops 1007288320 | bytes 4947968 | tf_op jit(solution)/shard_map/dot_general | solution.py:224
  134.4 0.0 copy-done.7
  134.4 0.3 copy-done.8
  134.7 1.5 fusion.12
  136.2 0.4 copy-done.1
  136.6 1.4 fusion.3
  138.0 1.8 fusion.2
  139.8 3.9 %all-to-all-start.1 = ((bf16[4,80,4224]{2,1,0:T(8,128)(2,1)}), bf16[4,80,4224]{2,1,0:T(8,128)(2,1)S(1)}, u32[]{:S(2)}, u32[]{:S(2)}) async-start(bf16[4,80,4224]{2,1,0:T(8,128)(2,1)} %bitcast.47), calls=%async_computation.1 | async-start | bytes 5406720 | tf_op jit(solution)/shard_map/all_to_all | solution.py:324
  143.7 0.1 fusion.18
  143.8 32.1 %all-to-all-done.1 = bf16[4,80,4224]{2,1,0:T(8,128)(2,1)S(1)} async-done(((bf16[4,80,4224]{2,1,0:T(8,128)(2,1)}), bf16[4,80,4224]{2,1,0:T(8,128)(2,1)S(1)}, u32[]{:S(2)}, u32[]{:S(2)}) %all-to-all-start.1) | async-done | bytes 2703392 | tf_op jit(solution)/shard_map/all_to_all | solution.py:324
  175.9 1.0 copy.72
  177.0 0.3 copy.73
  177.3 3.5 %convolution_convert_fusion.part_ref = bf16[16,32,4224]{2,1,0:T(8,128)(2,1)} fusion(bf16[16,20,4224]{2,0,1:T(8,128)(2,1)S(1)} %bitcast.46, pred[16,32,20]{1,0,2:T(8,128)(4,1)S(1)} %fusion.18), kind=kOutput, calls=%fused_computation | convolution fusion | flops 88670208 | bytes 7038976 | tf_op jit(solution)/shard_map/dot_general | solution.py:333
  180.7 53.8 %shard_map.103 = bf16[32,4224]{1,0:T(8,128)(2,1)} custom-call(bf16[16,32,4224]{2,1,0:T(8,128)(2,1)} %convolution_convert_fusion.part_ref), custom_call_target="tpu_custom_call" | custom-call | bytes 100000000 | tf_op jit(solution)/shard_map/pallas_call | solution.py:205
  234.5 0.7 slice_convert_fusion.1
  235.2 0.1 slice_add_fusion
  235.3 0.7 copy.76
  236.0 1.7 fusion.41
  (22 shorter events, 0.1 us)
Async XLA Ops:
  81.4 37.7 %all-to-all-start = ((bf16[4,80,4224]{2,1,0:T(8,128)(2,1)}), bf16[4,80,4224]{2,1,0:T(8,128)(2,1)S(1)}, u32[]{:S(2)}, u32[]{:S(2)}) async-start(bf16[4,80,4224]{2,1,0:T(8,128)(2,1)} %copy.69), calls=%async_computation | async-start | bytes 5406720 | tf_op jit(solution)/shard_map/all_to_all | solution.py:290
  85.7 152.0 %reduce-scatter.2.cloned.1.call-start = ((), (), s32[]{:S(2)}) async-start(), calls=%async_computation.3 | async-start | bytes 3538944 | tf_op jit(solution)/shard_map/reduce_scatter | solution.py:328
  119.3 3.2 %copy-start.2 = (bf16[8,256,768]{2,1,0:T(8,128)(2,1)S(1)}, bf16[8,256,768]{2,1,0:T(8,128)(2,1)}, u32[]{:S(2)}) copy-start(bf16[8,256,768]{2,1,0:T(8,128)(2,1)} %get-tuple-element.9) | copy-start | bytes 9437188
  122.5 1.3 copy-start.4
  122.5 2.4 copy-start
  123.7 3.5 %copy-start.6 = (f32[320,768]{1,0:T(8,128)}, f32[320,768]{1,0:T(8,128)S(1)}, u32[]{:S(2)}) copy-start(f32[320,768]{1,0:T(8,128)S(1)} %fusion.9) | copy-start | bytes 2949124
  131.0 3.4 %copy-start.3 = (bf16[8,256,768]{2,1,0:T(8,128)(2,1)S(1)}, bf16[8,256,768]{2,1,0:T(8,128)(2,1)}, u32[]{:S(2)}) copy-start(bf16[8,256,768]{2,1,0:T(8,128)(2,1)} %get-tuple-element.9) | copy-start | bytes 9437188
  131.0 3.4 %copy-start.5 = (f32[320,768]{1,0:T(8,128)S(1)}, f32[320,768]{1,0:T(8,128)}, u32[]{:S(2)}) copy-start(f32[320,768]{1,0:T(8,128)} %copy-done.4) | copy-start | bytes 2949124
  131.0 3.4 %copy-start.7 = (f32[320,768]{1,0:T(8,128)S(1)}, f32[320,768]{1,0:T(8,128)}, u32[]{:S(2)}) copy-start(f32[320,768]{1,0:T(8,128)} %copy-done.6) | copy-start | bytes 2949124
  131.0 3.7 %copy-start.8 = (f32[320,768]{1,0:T(8,128)S(1)}, f32[320,768]{1,0:T(8,128)}, u32[]{:S(2)}) copy-start(f32[320,768]{1,0:T(8,128)} %get-tuple-element.44) | copy-start | bytes 2949124
  134.7 1.9 copy-start.1
  139.8 36.2 %all-to-all-start.1 = ((bf16[4,80,4224]{2,1,0:T(8,128)(2,1)}), bf16[4,80,4224]{2,1,0:T(8,128)(2,1)S(1)}, u32[]{:S(2)}, u32[]{:S(2)}) async-start(bf16[4,80,4224]{2,1,0:T(8,128)(2,1)} %bitcast.47), calls=%async_computation.1 | async-start | bytes 5406720 | tf_op jit(solution)/shard_map/all_to_all | solution.py:324
Sparse Core Ops, SparseCore 0:
  131.0 35.4 reduce-scatter.1

commit v3 on v2

v3 whole, which is shorter than its diff:
```python
import functools
import jax
import jax.numpy as jnp
from jax import lax
from jax.experimental import pallas as pl
from jax.experimental.pallas import tpu as pltpu
from jax.sharding import PartitionSpec as P

NX = 4
NC = 2
TAIL = 128
SLOTS = 5
TILE = 16
BLOCK = 32
ORDER = (0, 1, -1, 2, -2, 3, -3, 4, -4, 5, -5, 6, -6, 7, -7, 8)
GROUP = 3
GROUPS = -(-len(ORDER) // GROUP)
COLUMNS = 384


MESH = pl.DeviceIdType.MESH


def contract_last(left, right):
    return lax.dot_general(
        left, right, (((1,), (1,)), ((), ())), preferred_element_type=jnp.float32
    )


def contract_first(left, right):
    return lax.dot_general(
        left, right, (((0,), (0,)), ((), ())), preferred_element_type=jnp.float32
    )


def three_parts(value):
    high = lax.reduce_precision(value, 8, 7)
    rest = value - high
    middle = lax.reduce_precision(rest, 8, 7)
    low = rest - middle
    return [part.astype(jnp.bfloat16) for part in (high, middle, low)]


def tail_of(parts):
    columns = jnp.concatenate(parts, axis=1)
    return jnp.pad(columns, ((0, 0), (0, TAIL - columns.shape[1])))


def ring_ends(nz):
    me = lax.axis_index("expert")
    z, x = me // NX, me % NX
    right = lax.rem(z + 1, nz) * NX + x
    left = lax.rem(z + nz - 1, nz) * NX + x
    return z, ({"expert": right}, {"expert": left})


def greet(others):
    barrier = pltpu.get_barrier_semaphore()
    for other in others:
        pl.semaphore_signal(barrier, inc=1, device_id=other, device_id_type=MESH)
    pl.semaphore_wait(barrier, len(others))


def x_peers():
    me = lax.axis_index("expert")
    z, x = me // NX, me % NX
    there = [lax.rem(x + step, NX) for step in range(1, NX)]
    return x, there, tuple({"expert": z * NX + other} for other in there)


def rows_of(distance, chunk):
    place = ORDER.index(8 if distance == -8 else distance)
    return pl.ds(place * BLOCK + chunk * TILE, TILE)


def group_rows(group):
    start = group * GROUP * BLOCK
    return pl.ds(start, min(GROUP * BLOCK, len(ORDER) * BLOCK - start))


def one_hots(tail, z, top_count):
    count = tail.shape[0]
    lanes = NX * TILE
    lane = lax.broadcasted_iota(jnp.int32, (count, lanes), 1)
    token = lax.broadcasted_iota(jnp.int32, (count, lanes), 0)
    expert = (z * NX + (lane >> 4)).astype(jnp.float32)
    match = jnp.zeros((count, lanes), jnp.float32)
    for k in range(top_count):
        match = jnp.where(tail[:, k:k + 1] == expert, 1.0, match)
    row = lax.broadcasted_iota(jnp.int32, (count, count), 0)
    col = lax.broadcasted_iota(jnp.int32, (count, count), 1)
    before = jnp.where(((row >> 5) == (col >> 5)) & (col < row), 1.0, 0.0)
    rank = jnp.dot(
        before.astype(jnp.bfloat16), match.astype(jnp.bfloat16),
        preferred_element_type=jnp.float32,
    )
    place = ((lane & (TILE - 1)) - SLOTS * (token >> 5)).astype(jnp.float32)
    return jnp.where(rank == place, match, 0.0).astype(jnp.bfloat16)


def gather_kernel(
    nz, ny, top_count, own_ref, w0_ref, w1_ref, w2_ref,
    out_ref, sel_ref, g0_ref, g1_ref, g2_ref,
    blocks, tiles, local_sem, send_sem, recv_sem, wsend_sem, wrecv_sem, xsend_sem, xrecv_sem,
):
    z, ends = ring_ends(nz)
    x, there, peers = x_peers()
    dp = lax.axis_index("dp")
    y, core = dp // NC, dp % NC
    behind = (lax.rem(y + ny - 1, ny) * NC + core, lax.rem(y + 1, ny) * NC + core)
    across = lax.rem(y + 2, ny) * NC + core
    ahead = ({"dp": behind[1]}, {"dp": behind[0]})
    sibling = {"dp": y * NC + 1 - core}
    greet(ends + ahead + (sibling,) + peers)
    half = nz // 2
    full_width = own_ref.shape[1]
    owned = (w0_ref, w1_ref, w2_ref)
    filled = (g0_ref, g1_ref, g2_ref)
    wrows = w0_ref.shape[0]

    def weight(j, k):
        own, full = owned[j], filled[j]
        if k < 2:
            source, target, to = own, full.at[dp], ahead[k]
        elif k < 4:
            part = pl.ds((k - 2) * (wrows // 2), wrows // 2)
            source = target = full.at[behind[k - 2], part]
            to = ahead[k - 2]
        elif k == 4:
            source, target, to = own, full.at[dp], sibling
        elif k < 7:
            source = target = full.at[behind[k - 5]]
            to = sibling
        else:
            part = pl.ds((k - 7) * (wrows // 2), wrows // 2)
            source = target = full.at[across, part]
            to = sibling
        return pltpu.make_async_remote_copy(
            src_ref=source, dst_ref=target,
            send_sem=wsend_sem.at[j, k], recv_sem=wrecv_sem.at[j, k],
            device_id=to, device_id_type=MESH,
        )

    def copy(step, way, chunk):
        sign = -1 if way == 0 else 1
        source = own_ref if step == 0 else blocks
        part = pl.ds(chunk * TILE, TILE) if step == 0 else rows_of(sign * step, chunk)
        return pltpu.make_async_remote_copy(
            src_ref=source.at[part],
            dst_ref=blocks.at[rows_of(sign * (step + 1), chunk)],
            send_sem=send_sem.at[step, way, chunk],
            recv_sem=recv_sem.at[step, way, chunk],
            device_id=ends[way], device_id_type=MESH,
        )

    def tile_copy(group, k):
        return pltpu.make_async_remote_copy(
            src_ref=tiles.at[group, there[k]],
            dst_ref=out_ref.at[x, pl.ds(group * TILE, TILE)],
            send_sem=xsend_sem.at[group, k], recv_sem=xrecv_sem.at[group, k],
            device_id=peers[k], device_id_type=MESH,
        )

    def tile_keep(group):
        return pltpu.make_async_copy(
            tiles.at[group, x], out_ref.at[x, pl.ds(group * TILE, TILE)],
            local_sem.at[3 + group],
        )

    def route(group):
        part = group_rows(group)
        tail = blocks[part, pl.ds(full_width - TAIL, TAIL)].astype(jnp.float32)
        sel = one_hots(tail, z, top_count)
        sel_ref[part, :] = sel

        def pick(i, carry):
            cut = pl.ds(pl.multiple_of(i * COLUMNS, 128), COLUMNS)
            picked = contract_first(sel, blocks[part, cut]).astype(jnp.bfloat16)
            tiles[group, :, :, cut] = picked.reshape(NX, TILE, COLUMNS)
            return carry

        lax.fori_loop(0, full_width // COLUMNS, pick, 0)
        for k in range(NX - 1):
            tile_copy(group, k).start()
        tile_keep(group).start()

    keep = [
        pltpu.make_async_copy(owned[j], filled[j].at[dp], local_sem.at[j]) for j in range(3)
    ]
    lanes = [(way, chunk) for chunk in range(2) for way in range(2)]
    for step in range(half):
        for way, chunk in lanes:
            if step > 0:
                copy(step - 1, way, chunk).wait_recv()
            if step < half - 1 or chunk == way:
                copy(step, way, chunk).start()
        if step == 0:
            for j in range(3):
                for k in (0, 1):
                    weight(j, k).start()
            for j in range(3):
                weight(j, 4).start()
            for one in keep:
                one.start()
            blocks[pl.ds(0, BLOCK), :] = own_ref[...]
        group = {1: 0, 3: 1, 4: 2, 6: 3, 7: 4}.get(step)
        if group is not None:
            route(group)
        j = {2: 0, 4: 1, 5: 2}.get(step)
        if j is not None:
            for k in range(2):
                weight(j, k).wait_recv()
                weight(j, 2 + k).start()
                weight(j, 5 + k).start()
        if step == half - 1:
            for j in range(2):
                for k in range(2):
                    weight(j, 2 + k).wait_recv()
                    weight(j, 7 + k).start()
    for way in range(2):
        copy(half - 1, way, way).wait_recv()
    route(GROUPS - 1)
    for k in range(2):
        weight(2, 2 + k).wait_recv()
        weight(2, 7 + k).start()
    for j in range(3):
        for k in range(4, 9):
            weight(j, k).wait_recv()
    for j in range(3):
        for k in range(9):
            weight(j, k).wait_send()
    for step in range(half):
        for way, chunk in lanes:
            if step < half - 1 or chunk == way:
                copy(step, way, chunk).wait_send()
    for group in range(GROUPS):
        for k in range(NX - 1):
            tile_copy(group, k).wait_recv()
            tile_copy(group, k).wait_send()
        tile_keep(group).wait()
    for one in keep:
        one.wait()


def ring_gather(payload, weights, nz, ny, top_count):
    rows, full = payload.shape
    half = nz // 2
    shards = [jax.ShapeDtypeStruct((ny * NC,) + w.shape, w.dtype) for w in weights]
    return pl.pallas_call(
        functools.partial(gather_kernel, nz, ny, top_count),
        out_shape=[
            jax.ShapeDtypeStruct((NX, GROUPS * TILE, full), payload.dtype),
            jax.ShapeDtypeStruct((nz * rows, NX * TILE), payload.dtype),
        ] + shards,
        in_specs=[pl.BlockSpec(memory_space=pltpu.VMEM)] * 4,
        out_specs=[
            pl.BlockSpec(memory_space=pl.ANY), pl.BlockSpec(memory_space=pltpu.VMEM)
        ] + [pl.BlockSpec(memory_space=pl.ANY)] * 3,
        scratch_shapes=[
            pltpu.VMEM((nz * rows, full), payload.dtype),
            pltpu.VMEM((GROUPS, NX, TILE, full), payload.dtype),
            pltpu.SemaphoreType.DMA((3 + GROUPS,)),
            pltpu.SemaphoreType.DMA((half, 2, 2)),
            pltpu.SemaphoreType.DMA((half, 2, 2)),
            pltpu.SemaphoreType.DMA((3, 9)),
            pltpu.SemaphoreType.DMA((3, 9)),
            pltpu.SemaphoreType.DMA((GROUPS, NX - 1)),
            pltpu.SemaphoreType.DMA((GROUPS, NX - 1)),
        ],
        compiler_params=pltpu.CompilerParams(collective_id=0, has_side_effects=True),
    )(payload, *weights)


def reduce_kernel(
    nz, back_ref, sel_ref, out_ref, landed, parts, held, going,
    local_sem, send_sem, recv_sem, xsend_sem, xrecv_sem,
):
    z, ends = ring_ends(nz)
    x, there, peers = x_peers()
    greet(ends + peers)
    half = nz // 2
    full_width = out_ref.shape[1]

    def tile_copy(group, k):
        return pltpu.make_async_remote_copy(
            src_ref=back_ref.at[there[k], pl.ds(group * TILE, TILE)],
            dst_ref=landed.at[group, x],
            send_sem=xsend_sem.at[group, k], recv_sem=xrecv_sem.at[group, k],
            device_id=peers[k], device_id_type=MESH,
        )

    def tile_keep(group):
        return pltpu.make_async_copy(
            back_ref.at[x, pl.ds(group * TILE, TILE)], landed.at[group, x],
            local_sem.at[group],
        )

    def add_up(group):
        for k in range(NX - 1):
            tile_copy(group, k).wait_recv()
        tile_keep(group).wait()
        part = group_rows(group)
        sel = sel_ref[part, :]

        def spread(i, carry):
            cut = pl.ds(pl.multiple_of(i * COLUMNS, 128), COLUMNS)
            rows = landed[group, :, :, cut].reshape(NX * TILE, COLUMNS)
            parts[part, cut] = jnp.dot(
                sel, rows, preferred_element_type=jnp.float32
            ).astype(jnp.bfloat16)
            return carry

        lax.fori_loop(0, full_width // COLUMNS, spread, 0)

    def copy(step, way, chunk):
        return pltpu.make_async_remote_copy(
            src_ref=going.at[step, way, chunk],
            dst_ref=held.at[step, way, chunk],
            send_sem=send_sem.at[step, way, chunk],
            recv_sem=recv_sem.at[step, way, chunk],
            device_id=ends[way], device_id_type=MESH,
        )

    def first(way, chunk):
        return 0 if chunk == way else 1

    for group in reversed(range(GROUPS)):
        for k in range(NX - 1):
            tile_copy(group, k).start()
        tile_keep(group).start()
    add_up(GROUPS - 1)
    lanes = [(way, chunk) for chunk in range(2) for way in range(2)]
    for step in range(half):
        for way, chunk in sorted(lanes, key=lambda lane: lane[0] != lane[1]):
            start = first(way, chunk)
            if step < start:
                continue
            distance = half - step
            value = parts[rows_of(distance if way == 0 else -distance, chunk), :]
            if step > start:
                copy(step - 1, way, chunk).wait_recv()
                value = (
                    value.astype(jnp.float32)
                    + held[step - 1, way, chunk].astype(jnp.float32)
                ).astype(value.dtype)
            going[step, way, chunk] = value
            copy(step, way, chunk).start()
        group = {0: 4, 1: 3, 3: 2, 4: 1, 6: 0}.get(step)
        if group is not None:
            add_up(group)
    for chunk in range(2):
        total = parts[rows_of(0, chunk), :].astype(jnp.float32)
        for way in range(2):
            copy(half - 1, way, chunk).wait_recv()
            total = total + held[half - 1, way, chunk].astype(jnp.float32)
        out_ref[pl.ds(chunk * TILE, TILE), :] = total.astype(out_ref.dtype)
    for step in range(half):
        for way, chunk in lanes:
            if step >= first(way, chunk):
                copy(step, way, chunk).wait_send()
    for group in range(GROUPS):
        for k in range(NX - 1):
            tile_copy(group, k).wait_send()


def ring_reduce(back, sel, nz):
    full = back.shape[2]
    rows = sel.shape[0] // nz
    half = nz // 2
    slots = (half, 2, 2, TILE, full)
    return pl.pallas_call(
        functools.partial(reduce_kernel, nz),
        out_shape=jax.ShapeDtypeStruct((rows, full), back.dtype),
        in_specs=[pl.BlockSpec(memory_space=pltpu.VMEM)] * 2,
        out_specs=pl.BlockSpec(memory_space=pltpu.VMEM),
        scratch_shapes=[
            pltpu.VMEM((GROUPS, NX, TILE, full), back.dtype),
            pltpu.VMEM((nz * rows, full), back.dtype),
            pltpu.VMEM(slots, back.dtype),
            pltpu.VMEM(slots, back.dtype),
            pltpu.SemaphoreType.DMA((GROUPS,)),
            pltpu.SemaphoreType.DMA((half, 2, 2)),
            pltpu.SemaphoreType.DMA((half, 2, 2)),
            pltpu.SemaphoreType.DMA((GROUPS, NX - 1)),
            pltpu.SemaphoreType.DMA((GROUPS, NX - 1)),
        ],
        compiler_params=pltpu.CompilerParams(collective_id=1, has_side_effects=True),
    )(back, sel)


def on_device(tokens, route_weight, upstream, expert_index, gate_weight, up_weight, down_weight):
    n_experts = lax.axis_size("expert")
    nz = n_experts // NX
    top_count = expert_index.shape[1]
    width = tokens.shape[1]
    me = lax.axis_index("expert")
    ny = lax.axis_size("dp") // NC
    payload = jnp.concatenate(
        [tokens, upstream,
         tail_of([expert_index.astype(jnp.bfloat16)] + three_parts(route_weight))],
        axis=1,
    )
    full = payload.shape[1]
    arrived, sel, *shards = ring_gather(
        payload, (gate_weight[0], up_weight[0], down_weight[0]), nz, ny, top_count
    )
    w_gate, w_up, w_down = (one.reshape(width, -1) for one in shards)
    arrived = arrived.reshape(NX * GROUPS * TILE, full)

    routed_tokens = arrived[:, :width]
    routed_up = arrived[:, width:2 * width]
    tail = arrived[:, 2 * width:].astype(jnp.float32)
    place = tail[:, :top_count] == me.astype(jnp.float32)
    weights = (
        tail[:, top_count:2 * top_count]
        + tail[:, 2 * top_count:3 * top_count]
        + tail[:, 3 * top_count:4 * top_count]
    )
    weight = jnp.sum(jnp.where(place, weights, 0.0), axis=1, keepdims=True)

    gate_value = jnp.dot(routed_tokens, w_gate, preferred_element_type=jnp.float32)
    up_value = jnp.dot(routed_tokens, w_up, preferred_element_type=jnp.float32)
    sig = jax.nn.sigmoid(gate_value)
    activated = gate_value * sig
    slope = sig * (1.0 + gate_value * (1.0 - sig))
    hidden_f = activated * up_value
    hidden = hidden_f.astype(jnp.bfloat16)
    raw_grad = jnp.dot(routed_up, w_down, preferred_element_type=jnp.float32)
    route_value = jnp.sum(hidden.astype(jnp.float32) * raw_grad, axis=1, keepdims=True)
    hidden_grad = raw_grad * weight
    weighted_hidden = (hidden_f * weight).astype(jnp.bfloat16)
    gate_grad = (hidden_grad * up_value * slope).astype(jnp.bfloat16)
    up_grad = (hidden_grad * activated).astype(jnp.bfloat16)
    out_rows = contract_last(weighted_hidden, w_down).astype(jnp.bfloat16)
    row_grad = (contract_last(gate_grad, w_gate) + contract_last(up_grad, w_up)).astype(
        jnp.bfloat16
    )
    route_tail = tail_of(three_parts(jnp.where(place, route_value, 0.0)))
    back = jnp.concatenate([out_rows, row_grad, route_tail], axis=1)
    down_grad = lax.psum_scatter(
        contract_first(routed_up, weighted_hidden).astype(jnp.bfloat16),
        "dp", scatter_dimension=0, tiled=True,
    )[None]
    summed = ring_reduce(back.reshape(NX, GROUPS * TILE, full), sel, nz)
    combined = summed[:, :width]
    token_grad = summed[:, width:2 * width]
    last = summed[:, 2 * width:].astype(jnp.float32)
    route_grad = (
        last[:, :top_count] + last[:, top_count:2 * top_count] + last[:, 2 * top_count:3 * top_count]
    )
    return (combined, token_grad, route_grad, down_grad)


def solution(mesh):
    return jax.shard_map(
        on_device,
        mesh=mesh,
        in_specs=(
            P(("dp", "expert"), None),
            P(("dp", "expert"), None),
            P(("dp", "expert"), None),
            P(("dp", "expert"), None),
            P("expert", "dp", None),
            P("expert", "dp", None),
            P("expert", "dp", None),
        ),
        out_specs=(
            P(("dp", "expert"), None),
            P(("dp", "expert"), None),
            P(("dp", "expert"), None),
            P("expert", "dp", None),
        ),
        check_vma=False,
    )
```

time: 246 us -> 184 us (0.75)
  waiting for transfers between devices: 65.5 us -> 0.02 us
  Pallas kernels: 116 us -> 139 us
  starting transfers between devices: 8.24 us -> 0.04 us
  matrix products: 23.4 us -> 18.5 us
  local copies, waits for them, and re-layouts: 10 us -> 6.47 us
    all_to_all x2 -> x0, waiting for transfers between devices: 65.5 us -> none  [the longest x1 33.4 us: on_device(): lax.all_to_all(rows, 'expert', split_axis=0, concat_axis=0, tiled=True, a...]
    pallas_call x1, Pallas kernels: 53.8 us -> 66 us  [ring_reduce(): pl.pallas_call(functools.partial(reduce_kernel, nz), out_shape=jax.ShapeD...]
    pallas_call x1, Pallas kernels: 62.2 us -> 72.7 us  [ring_gather(): pl.pallas_call(functools.partial(gather_kernel, nz, ny, top_count), out_s...]
    all_to_all x2 -> x0, starting transfers between devices: 8.24 us -> none  [the longest x1 4.29 us: on_device(): lax.all_to_all(rows, 'expert', split_axis=0, concat_axis=0, tiled=True, a...]
    dot_general x3 -> x0, matrix products: 6.85 us -> none  [the longest x1 3.48 us: on_device(): lax.dot_general(sel.transpose(1, 3, 0, 2).reshape(nz, tok_count, NX * cap...]
    dot_general x1, matrix products: 1.2 us -> 3.89 us  [on_device(): jnp.dot(routed_tokens, w_gate, preferred_element_type=jnp.float32)]
  transfers between devices with their start and end apart: 3 -> 1, of which waited for: 2 -> 0; matrix products, arithmetic and copies ran while one was open for 7% -> 7% of each run, Pallas kernels for 22% -> 36%
where the time goes in v3:
time: 184 us
  Pallas kernels  139 us (76%)
  matrix products  18.5 us (10%)
  between operations  14.2 us (8%)
  local copies, waits for them, and re-layouts  6.47 us (4%)
  other arithmetic  5.84 us (3%)
    pallas_call x1, Pallas kernels, ring_gather(): pl.pallas_call(functools.partial(gather_kernel, nz, ny, top_count), out_s...  72.7 us
    pallas_call x1, Pallas kernels, ring_reduce(): pl.pallas_call(functools.partial(reduce_kernel, nz), out_shape=jax.ShapeD...  66 us
    dot_general x3, matrix products, contract_last(): lax.dot_general(left, right, (((1,), (1,)), ((), ())), preferred_element_...  7.03 us
    dot_general x1, matrix products, on_device(): jnp.dot(routed_tokens, w_gate, preferred_element_type=jnp.float32)  3.89 us
  transfers between devices with their start and end apart: 1, of which 0 were waited for; matrix products, arithmetic and copies ran while one was open for 7% of the time, Pallas kernels for 36%

profile of v3, /device:TPU:24, one launch (start us, length us, event | category | flops | bytes accessed | tf_op | source)
XLA Modules:
  0.0 183.8 jit_solution(13375117163760076327)
XLA Ops:
  7.2 0.0 reduce-scatter.2.cloned.1.call-start
  7.2 0.7 reduce_precision.12
  7.9 0.8 copy.22
  8.7 0.7 convert_element_type.58
  9.4 0.1 copy.24
  9.4 0.1 copy.21
  9.5 0.1 fusion.24
  9.6 1.7 pad_maximum_fusion.own_ref
  11.3 72.7 %shard_map.102 = (bf16[4,96,4224]{2,1,0:T(8,128)(2,1)}, bf16[512,64]{1,0:T(8,128)(2,1)}, bf16[8,256,768]{2,1,0:T(8,128)(2,1)}, bf16[8,256,768]{2,1,0:T(8,128)(2,1)}, bf16[8,256,768]{2,1,0:T(8,128)(2,1)}) custom-call(bf16[32,4224]{1,0:T(8,128)(2,1)} %pad_maximum_fusion.own_ref, bf16[256,768]{1,0:T(8,128)(2,1)} %bitcast.18, bf16[256,768]{1,0:T(8,128)(2,1)} %bitcast.19, ...), custom_call_target="tpu_custom_call" | custom-call | tf_op jit(solution)/shard_map/pallas_call | solution.py:249
  84.0 0.9 slice.53
  84.9 0.1 copy.28
  85.1 0.0 copy-start
  85.1 0.0 copy-start.3
  85.1 3.9 %fusion.7 = f32[384,768]{1,0:T(8,128)S(1)} fusion(bf16[2048,768]{1,0:T(8,128)(2,1)} %bitcast.28, bf16[384,4224]{1,0:T(8,128)(2,1)} %bitcast.22), kind=kOutput, calls=%fused_computation.11 | convolution fusion | flops 1207959552 | bytes 5898240 | tf_op jit(solution)/shard_map/dot_general | solution.py:421
  89.0 0.0 copy-start.4
  89.0 0.0 copy-done
  89.0 0.4 copy-done.3
  89.4 0.0 copy-start.1
  89.4 1.4 fusion.3
  90.8 0.0 copy-start.6
  90.8 0.0 copy-done.4
  90.9 0.5 copy-done.1
  91.3 2.6 %multiply_convert_fusion.2 = (bf16[384,768]{1,0:T(8,128)(2,1)S(1)}, f32[384]{0:T(512)S(1)}, f32[384,768]{1,0:T(8,128)}) fusion(f32[384]{0:T(512)S(1)} %get-tuple-element.26, f32[384,768]{1,0:T(8,128)S(1)} %fusion.7, f32[384,768]{1,0:T(8,128)S(1)} %fusion.3, bf16[2048,768]{1,0:T(8,128)(2,1)S(1)} %bitcast.26, bf16[384,4224]{1,0:T(8,128)(2,1)S(1)} %bitcast.24), kind=kOutput, calls=%fused_computation.16 | convolution fusion | flops 1211203200 | bytes 8850944 | tf_op jit(solution)/shard_map/dot_general | solution.py:422
  93.9 0.0 copy-done.6
  93.9 0.0 copy-start.8
  93.9 0.8 copy-done.8
  94.8 3.5 %convolution_convert_fusion = bf16[2048,768]{1,0:T(8,128)(2,1)} fusion(bf16[384,768]{1,0:T(8,128)(2,1)S(1)} %get-tuple-element.28, bf16[384,4224]{1,0:T(8,128)(2,1)S(1)} %bitcast.25), kind=kOutput, calls=%fused_computation.2 | convolution fusion | flops 1209532416 | bytes 5308416 | tf_op jit(solution)/shard_map/dot_general | solution.py:31
  98.3 0.0 reduce-scatter.2.cloned.1.call-update
  98.4 0.1 copy.26
  98.5 0.0 copy-start.2
  98.5 0.0 copy-start.5
  98.5 0.0 copy-start.7
  98.5 0.0 copy-start.9
  98.5 3.6 %convolution_convert_fusion.1 = bf16[384,2048]{1,0:T(8,128)(2,1)S(1)} fusion(bf16[384,768]{1,0:T(8,128)(2,1)} %copy-done.8, bf16[2048,768]{1,0:T(8,128)(2,1)} %bitcast.30), kind=kOutput, calls=%fused_computation.5 | convolution fusion | flops 1208745984 | bytes 5308416 | tf_op jit(solution)/shard_map/dot_general | solution.py:25
  102.2 0.0 copy-done.2
  102.2 0.0 copy-done.5
  102.2 0.0 copy-done.7
  102.2 0.3 copy-done.9
  102.6 1.7 fusion.10
  104.3 1.7 add_convert_fusion
  106.0 1.8 fusion.1
  107.8 66.0 %shard_map.103 = bf16[32,4224]{1,0:T(8,128)(2,1)} custom-call(bf16[4,96,4224]{2,1,0:T(8,128)(2,1)} %bitcast.17, bf16[512,64]{1,0:T(8,128)(2,1)} %get-tuple-element.13.sel_ref), custom_call_target="tpu_custom_call" | custom-call | tf_op jit(solution)/shard_map/pallas_call | solution.py:371
  173.8 0.7 slice_convert_fusion
  174.5 0.1 slice_add_fusion
  174.6 0.7 copy.27
  175.3 1.7 fusion.27
  176.9 0.0 reduce-scatter.2.cloned.1.call-done
  (5 shorter events, 0.1 us)
Async XLA Ops:
  7.2 169.8 %reduce-scatter.2.cloned.1.call-start = ((), (), s32[]{:S(2)}) async-start(), calls=%async_computation.1 | async-start | bytes 3538944 | tf_op jit(solution)/shard_map/reduce_scatter | solution.py:440
  85.1 3.9 %copy-start = (bf16[4,96,4224]{2,1,0:T(8,128)(2,1)S(1)}, bf16[4,96,4224]{2,1,0:T(8,128)(2,1)}, u32[]{:S(2)}) copy-start(bf16[4,96,4224]{2,1,0:T(8,128)(2,1)} %get-tuple-element.9) | copy-start | bytes 9732100
  85.1 4.3 %copy-start.3 = (bf16[8,256,768]{2,1,0:T(8,128)(2,1)S(1)}, bf16[8,256,768]{2,1,0:T(8,128)(2,1)}, u32[]{:S(2)}) copy-start(bf16[8,256,768]{2,1,0:T(8,128)(2,1)} %get-tuple-element.12) | copy-start | bytes 9437188
  89.0 1.8 %copy-start.4 = (f32[384,768]{1,0:T(8,128)}, f32[384,768]{1,0:T(8,128)S(1)}, u32[]{:S(2)}) copy-start(f32[384,768]{1,0:T(8,128)S(1)} %fusion.7) | copy-start | bytes 3538948
  89.4 1.9 %copy-start.1 = (bf16[8,256,768]{2,1,0:T(8,128)(2,1)S(1)}, bf16[8,256,768]{2,1,0:T(8,128)(2,1)}, u32[]{:S(2)}) copy-start(bf16[8,256,768]{2,1,0:T(8,128)(2,1)} %get-tuple-element.11) | copy-start | bytes 9437188
  90.8 3.1 %copy-start.6 = (f32[384,768]{1,0:T(8,128)}, f32[384,768]{1,0:T(8,128)S(1)}, u32[]{:S(2)}) copy-start(f32[384,768]{1,0:T(8,128)S(1)} %fusion.3) | copy-start | bytes 3538948
  93.9 0.8 copy-start.8
  98.5 3.7 %copy-start.2 = (bf16[8,256,768]{2,1,0:T(8,128)(2,1)S(1)}, bf16[8,256,768]{2,1,0:T(8,128)(2,1)}, u32[]{:S(2)}) copy-start(bf16[8,256,768]{2,1,0:T(8,128)(2,1)} %get-tuple-element.10) | copy-start | bytes 9437188
  98.5 3.7 %copy-start.5 = (f32[384,768]{1,0:T(8,128)S(1)}, f32[384,768]{1,0:T(8,128)}, u32[]{:S(2)}) copy-start(f32[384,768]{1,0:T(8,128)} %copy-done.4) | copy-start | bytes 3538948
  98.5 3.7 %copy-start.7 = (f32[384,768]{1,0:T(8,128)S(1)}, f32[384,768]{1,0:T(8,128)}, u32[]{:S(2)}) copy-start(f32[384,768]{1,0:T(8,128)} %copy-done.6) | copy-start | bytes 3538948
  98.5 4.0 %copy-start.9 = (f32[384,768]{1,0:T(8,128)S(1)}, f32[384,768]{1,0:T(8,128)}, u32[]{:S(2)}) copy-start(f32[384,768]{1,0:T(8,128)} %get-tuple-element.38) | copy-start | bytes 3538948
Sparse Core Ops, SparseCore 0:
  98.5 36.4 reduce-scatter.1

commit v4 on v3

--- a/solution.py
+++ b/solution.py
@@ -66,6 +66,14 @@
     z, x = me // NX, me % NX
     there = [lax.rem(x + step, NX) for step in range(1, NX)]
     return x, there, tuple({"expert": z * NX + other} for other in there)
+
+
+def dp_ends(ny):
+    dp = lax.axis_index("dp")
+    y, core = dp // NC, dp % NC
+    behind = (lax.rem(y + ny - 1, ny) * NC + core, lax.rem(y + 1, ny) * NC + core)
+    ahead = ({"dp": behind[1]}, {"dp": behind[0]})
+    return dp, y, core, behind, ahead, {"dp": y * NC + 1 - core}
 
 
 def rows_of(distance, chunk):
@@ -105,12 +113,8 @@
 ):
     z, ends = ring_ends(nz)
     x, there, peers = x_peers()
-    dp = lax.axis_index("dp")
-    y, core = dp // NC, dp % NC
-    behind = (lax.rem(y + ny - 1, ny) * NC + core, lax.rem(y + 1, ny) * NC + core)
+    dp, y, core, behind, ahead, sibling = dp_ends(ny)
     across = lax.rem(y + 2, ny) * NC + core
-    ahead = ({"dp": behind[1]}, {"dp": behind[0]})
-    sibling = {"dp": y * NC + 1 - core}
     greet(ends + ahead + (sibling,) + peers)
     half = nz // 2
     full_width = own_ref.shape[1]
@@ -272,14 +276,91 @@
 
 
 def reduce_kernel(
-    nz, back_ref, sel_ref, out_ref, landed, parts, held, going,
-    local_sem, send_sem, recv_sem, xsend_sem, xrecv_sem,
+    nz, ny, back_ref, sel_ref, down_ref, out_ref, grad_ref, landed, parts, held, going,
+    paired, far, near, far_held, near_held,
+    local_sem, send_sem, recv_sem, xsend_sem, xrecv_sem, dsend_sem, drecv_sem,
 ):
     z, ends = ring_ends(nz)
     x, there, peers = x_peers()
-    greet(ends + peers)
+    dp, y, core, behind, ahead, sibling = dp_ends(ny)
+    greet(ends + peers + ahead + (sibling,))
     half = nz // 2
     full_width = out_ref.shape[1]
+    drows = grad_ref.shape[0] // 2
+
+    def owner(turn, side):
+        return lax.rem(y + turn, ny) * NC + side
+
+    def down_copy(k):
+        if k < ny:
+            source, target, to = down_ref.at[owner(k, 1 - core)], paired.at[k], sibling
+        elif k < ny + 2:
+            way = k - ny
+            source, target, to = far.at[way], far_held.at[way], ahead[way]
+        else:
+            way = k - ny - 2
+            source, target, to = near.at[way], near_held.at[way], ahead[way]
+        return pltpu.make_async_remote_copy(
+            src_ref=source, dst_ref=target,
+            send_sem=dsend_sem.at[k], recv_sem=drecv_sem.at[k],
+            device_id=to, device_id_type=MESH,
+        )
+
+    def pair_sum(turn, piece):
+        part = pl.ds(piece * TILE, TILE)
+        return (
+            down_ref[owner(turn, core), part, :].astype(jnp.float32)
+            + paired[turn, part, :].astype(jnp.float32)
+        )
+
+    pieces = drows // TILE
+
+    def down_far():
+        down_copy(2).wait_recv()
+        for way in range(2):
+            def body(i, carry, way=way):
+                far[way, pl.ds(i * TILE, TILE), :] = pair_sum(2, way * pieces + i).astype(far.dtype)
+                return carry
+
+            lax.fori_loop(0, pieces, body, 0)
+            down_copy(ny + way).start()
+
+    def down_near():
+        for way, turn in ((0, 1), (1, 3)):
+            down_copy(turn).wait_recv()
+            down_copy(ny + way).wait_recv()
+
+            def relayed(i, carry, way=way, turn=turn):
+                part = pl.ds((way * pieces + i) * TILE, TILE)
+                near[way, part, :] = (
+                    pair_sum(turn, way * pieces + i)
+                    + far_held[way, pl.ds(i * TILE, TILE), :].astype(jnp.float32)
+                ).astype(near.dtype)
+                return carry
+
+            def plain(i, carry, way=way, turn=turn):
+                at = (1 - way) * pieces + i
+                near[way, pl.ds(at * TILE, TILE), :] = pair_sum(turn, at).astype(near.dtype)
+                return carry
+
+            lax.fori_loop(0, pieces, relayed, 0)
+            lax.fori_loop(0, pieces, plain, 0)
+            down_copy(ny + 2 + way).start()
+
+    def down_last():
+        down_copy(0).wait_recv()
+        for way in range(2):
+            down_copy(ny + 2 + way).wait_recv()
+
+        def body(i, carry):
+            part = pl.ds(i * TILE, TILE)
+            total = pair_sum(0, i)
+            for way in range(2):
+                total = total + near_held[way, part, :].astype(jnp.float32)
+            grad_ref[part, :] = total.astype(grad_ref.dtype)
+            return carry
+
+        lax.fori_loop(0, 2 * pieces, body, 0)
 
     def tile_copy(group, k):
         return pltpu.make_async_remote_copy(
@@ -328,6 +409,9 @@
         for k in range(NX - 1):
             tile_copy(group, k).start()
         tile_keep(group).start()
+    for k in (2, 1, 3, 0):
+        down_copy(k).start()
+    down_far()
     add_up(GROUPS - 1)
     lanes = [(way, chunk) for chunk in range(2) for way in range(2)]
     for step in range(half):
@@ -348,6 +432,10 @@
         group = {0: 4, 1: 3, 3: 2, 4: 1, 6: 0}.get(step)
         if group is not None:
             add_up(group)
+        if step == 2:
+            down_near()
+        if step == 5:
+            down_last()
     for chunk in range(2):
         total = parts[rows_of(0, chunk), :].astype(jnp.float32)
         for way in range(2):
@@ -361,31 +449,44 @@
     for group in range(GROUPS):
         for k in range(NX - 1):
             tile_copy(group, k).wait_send()
-
-
-def ring_reduce(back, sel, nz):
+    for k in range(ny + 4):
+        down_copy(k).wait_send()
+
+
+def ring_reduce(back, sel, down, nz, ny):
     full = back.shape[2]
     rows = sel.shape[0] // nz
     half = nz // 2
     slots = (half, 2, 2, TILE, full)
+    drows, dcols = down.shape[1:]
     return pl.pallas_call(
-        functools.partial(reduce_kernel, nz),
-        out_shape=jax.ShapeDtypeStruct((rows, full), back.dtype),
-        in_specs=[pl.BlockSpec(memory_space=pltpu.VMEM)] * 2,
-        out_specs=pl.BlockSpec(memory_space=pltpu.VMEM),
+        functools.partial(reduce_kernel, nz, ny),
+        out_shape=[
+            jax.ShapeDtypeStruct((rows, full), back.dtype),
+            jax.ShapeDtypeStruct((drows, dcols), down.dtype),
+        ],
+        in_specs=[pl.BlockSpec(memory_space=pltpu.VMEM)] * 3,
+        out_specs=[pl.BlockSpec(memory_space=pltpu.VMEM)] * 2,
         scratch_shapes=[
             pltpu.VMEM((GROUPS, NX, TILE, full), back.dtype),
             pltpu.VMEM((nz * rows, full), back.dtype),
             pltpu.VMEM(slots, back.dtype),
             pltpu.VMEM(slots, back.dtype),
+            pltpu.VMEM((ny, drows, dcols), down.dtype),
+            pltpu.VMEM((2, drows // 2, dcols), down.dtype),
+            pltpu.VMEM((2, drows, dcols), down.dtype),
+            pltpu.VMEM((2, drows // 2, dcols), down.dtype),
+            pltpu.VMEM((2, drows, dcols), down.dtype),
             pltpu.SemaphoreType.DMA((GROUPS,)),
             pltpu.SemaphoreType.DMA((half, 2, 2)),
             pltpu.SemaphoreType.DMA((half, 2, 2)),
             pltpu.SemaphoreType.DMA((GROUPS, NX - 1)),
             pltpu.SemaphoreType.DMA((GROUPS, NX - 1)),
+            pltpu.SemaphoreType.DMA((ny + 4,)),
+            pltpu.SemaphoreType.DMA((ny + 4,)),
         ],
         compiler_params=pltpu.CompilerParams(collective_id=1, has_side_effects=True),
-    )(back, sel)
+    )(back, sel, down)
 
 
 def on_device(tokens, route_weight, upstream, expert_index, gate_weight, up_weight, down_weight):
@@ -437,18 +538,18 @@
     )
     route_tail = tail_of(three_parts(jnp.where(place, route_value, 0.0)))
     back = jnp.concatenate([out_rows, row_grad, route_tail], axis=1)
-    down_grad = lax.psum_scatter(
-        contract_first(routed_up, weighted_hidden).astype(jnp.bfloat16),
-        "dp", scatter_dimension=0, tiled=True,
-    )[None]
-    summed = ring_reduce(back.reshape(NX, GROUPS * TILE, full), sel, nz)
+    down_part = contract_first(routed_up, weighted_hidden).astype(jnp.bfloat16)
+    summed, down_grad = ring_reduce(
+        back.reshape(NX, GROUPS * TILE, full), sel,
+        down_part.reshape(ny * NC, -1, down_part.shape[1]), nz, ny,
+    )
     combined = summed[:, :width]
     token_grad = summed[:, width:2 * width]
     last = summed[:, 2 * width:].astype(jnp.float32)
     route_grad = (
         last[:, :top_count] + last[:, top_count:2 * top_count] + last[:, 2 * top_count:3 * top_count]
     )
-    return (combined, token_grad, route_grad, down_grad)
+    return (combined, token_grad, route_grad, down_grad[None])
 
 
 def solution(mesh):

time: 184 us -> 170 us (0.924)
  between operations: 14.2 us -> 0.76 us
  matrix products: 18.5 us -> 15.4 us
    dot_general x3, matrix products: 7.03 us -> 4.85 us  [contract_last(): lax.dot_general(left, right, (((1,), (1,)), ((), ())), preferred_element_...]
    unnamed x23 -> x12, local copies, waits for them, and re-layouts: 3.59 us -> 4.18 us
  transfers between devices with their start and end apart: 1 -> 0, of which waited for: 0 -> 0; matrix products, arithmetic and copies ran while one was open for 7% -> 0% of each run, Pallas kernels for 36% -> 0%
where the time goes in v4:
time: 170 us; the launch traced here: 169 us
  Pallas kernels  140 us (82%)
  matrix products  15.4 us (9%)
  local copies, waits for them, and re-layouts  7.06 us (4%)
  other arithmetic  5.79 us (3%)
    pallas_call x1, Pallas kernels, ring_gather(): pl.pallas_call(functools.partial(gather_kernel, nz, ny, top_count), out_s...  72.7 us
    pallas_call x1, Pallas kernels, ring_reduce(): pl.pallas_call(functools.partial(reduce_kernel, nz, ny), out_shape=[jax.S...  67.1 us
    dot_general x3, matrix products, contract_last(): lax.dot_general(left, right, (((1,), (1,)), ((), ())), preferred_element_...  4.85 us
    unnamed x12, local copies, waits for them, and re-layouts  4.18 us
    dot_general x1, matrix products, on_device(): jnp.dot(routed_tokens, w_gate, preferred_element_type=jnp.float32)  3.89 us
    dot_general x1, matrix products, contract_first(): lax.dot_general(left, right, (((0,), (0,)), ((), ())), preferred_element_...  3.56 us

profile of v4, /device:TPU:24, one launch (start us, length us, event | category | flops | bytes accessed | tf_op | source)
XLA Modules:
  0.0 168.8 jit_solution(8431678787158283556)
XLA Ops:
  0.6 0.7 convert_element_type.58
  1.3 0.7 reduce_precision.12
  2.0 0.1 copy.24
  2.1 0.1 copy.21
  2.2 0.8 copy.22
  3.0 0.1 fusion.24
  3.0 1.7 %pad_maximum_fusion.own_ref = bf16[32,4224]{1,0:T(8,128)(2,1)} fusion(bf16[32,128]{1,0:T(8,128)(2,1)S(1)} %fusion.24, bf16[32,2048]{1,0:T(8,128)(2,1)} %param.9, bf16[32,2048]{1,0:T(8,128)(2,1)} %param.7), kind=kLoop, calls=%fused_computation.23 | loop fusion | flops 811008 | bytes 540672 | tf_op jit(solution)/shard_map/concatenate | solution.py:499
  4.7 72.7 %shard_map.102 = (bf16[4,96,4224]{2,1,0:T(8,128)(2,1)}, bf16[512,64]{1,0:T(8,128)(2,1)}, bf16[8,256,768]{2,1,0:T(8,128)(2,1)}, bf16[8,256,768]{2,1,0:T(8,128)(2,1)}, bf16[8,256,768]{2,1,0:T(8,128)(2,1)}) custom-call(bf16[32,4224]{1,0:T(8,128)(2,1)} %pad_maximum_fusion.own_ref, bf16[256,768]{1,0:T(8,128)(2,1)} %bitcast.21, bf16[256,768]{1,0:T(8,128)(2,1)} %bitcast.22, ...), custom_call_target="tpu_custom_call" | custom-call | tf_op jit(solution)/shard_map/pallas_call | solution.py:253
  77.5 0.9 slice.53
  78.4 0.1 copy.28
  78.5 0.0 copy-start
  78.5 0.0 copy-start.3
  78.6 3.9 %fusion.7 = f32[384,768]{1,0:T(8,128)S(1)} fusion(bf16[2048,768]{1,0:T(8,128)(2,1)} %bitcast.31, bf16[384,4224]{1,0:T(8,128)(2,1)} %bitcast.25), kind=kOutput, calls=%fused_computation.11 | convolution fusion | flops 1207959552 | bytes 5898240 | tf_op jit(solution)/shard_map/dot_general | solution.py:522
  82.5 0.0 copy-done
  82.5 0.4 copy-done.3
  82.8 0.0 copy-start.1
  82.8 1.4 fusion.3
  84.2 0.5 copy-done.1
  84.7 1.7 multiply_convert_fusion.2
  86.4 1.4 convolution_convert_fusion.1
  87.8 0.0 copy-start.2
  87.8 3.6 %convolution_convert_fusion = bf16[2048,768]{1,0:T(8,128)(2,1)} fusion(bf16[384,768]{1,0:T(8,128)(2,1)S(1)} %get-tuple-element.32, bf16[384,4224]{1,0:T(8,128)(2,1)S(1)} %bitcast.28), kind=kOutput, calls=%fused_computation.2 | convolution fusion | flops 1209532416 | bytes 5308416 | tf_op jit(solution)/shard_map/dot_general | solution.py:31
  91.4 0.0 copy-done.2
  91.4 1.8 %fusion.10 = f32[384,2048]{1,0:T(8,128)S(1)} fusion(bf16[2048,768]{1,0:T(8,128)(2,1)S(1)} %bitcast.32, f32[384,768]{1,0:T(8,128)S(1)} %fusion.7, f32[384,768]{1,0:T(8,128)S(1)} %get-tuple-element.42, f32[384,768]{1,0:T(8,128)S(1)} %fusion.3, f32[384]{0:T(512)S(1)} %get-tuple-element.30), kind=kOutput, calls=%fused_computation.19 | convolution fusion | flops 1211203584 | bytes 9831936 | tf_op jit(solution)/shard_map/dot_general | solution.py:25
  93.1 1.7 add_convert_fusion
  94.9 0.1 copy.26
  95.0 1.8 %fusion.1 = bf16[384,4224]{1,0:T(8,128)(2,1)} fusion(bf16[384,24]{1,0:T(8,128)(2,1)S(1)} %copy.26, bf16[384,2048]{1,0:T(8,128)(2,1)S(1)} %add_convert_fusion, bf16[384,2048]{1,0:T(8,128)(2,1)S(1)} %convolution_convert_fusion.1), kind=kLoop, calls=%fused_computation.3 | loop fusion | flops 12976128 | bytes 6408192 | tf_op jit(solution)/shard_map/concatenate | solution.py:540
  96.8 67.1 %shard_map.103 = (bf16[32,4224]{1,0:T(8,128)(2,1)}, bf16[256,768]{1,0:T(8,128)(2,1)}) custom-call(bf16[4,96,4224]{2,1,0:T(8,128)(2,1)} %bitcast.18, bf16[512,64]{1,0:T(8,128)(2,1)} %get-tuple-element.15.sel_ref, bf16[8,256,768]{2,1,0:T(8,128)(2,1)} %bitcast.19), custom_call_target="tpu_custom_call" | custom-call | tf_op jit(solution)/shard_map/pallas_call | solution.py:462
  163.9 0.7 slice_convert_fusion
  164.6 1.7 fusion.27
  166.3 0.1 slice_add_fusion
  166.3 0.7 copy.27
  167.0 1.8 %copy.30 = bf16[1,256,768]{2,1,0:T(8,128)(2,1)} copy(bf16[1,256,768]{2,1,0:T(8,128)(2,1)} %bitcast.20) | data formatting | bytes 786432
  (5 shorter events, 0.1 us)
Async XLA Ops:
  78.5 3.9 %copy-start = (bf16[4,96,4224]{2,1,0:T(8,128)(2,1)S(1)}, bf16[4,96,4224]{2,1,0:T(8,128)(2,1)}, u32[]{:S(2)}) copy-start(bf16[4,96,4224]{2,1,0:T(8,128)(2,1)} %get-tuple-element.11) | copy-start | bytes 9732100
  78.5 4.3 %copy-start.3 = (bf16[8,256,768]{2,1,0:T(8,128)(2,1)S(1)}, bf16[8,256,768]{2,1,0:T(8,128)(2,1)}, u32[]{:S(2)}) copy-start(bf16[8,256,768]{2,1,0:T(8,128)(2,1)} %get-tuple-element.14) | copy-start | bytes 9437188
  82.8 1.9 %copy-start.1 = (bf16[8,256,768]{2,1,0:T(8,128)(2,1)S(1)}, bf16[8,256,768]{2,1,0:T(8,128)(2,1)}, u32[]{:S(2)}) copy-start(bf16[8,256,768]{2,1,0:T(8,128)(2,1)} %get-tuple-element.13) | copy-start | bytes 9437188
  87.8 3.6 %copy-start.2 = (bf16[8,256,768]{2,1,0:T(8,128)(2,1)S(1)}, bf16[8,256,768]{2,1,0:T(8,128)(2,1)}, u32[]{:S(2)}) copy-start(bf16[8,256,768]{2,1,0:T(8,128)(2,1)} %get-tuple-element.12) | copy-start | bytes 9437188

commit v5 on v4

--- a/solution.py
+++ b/solution.py
@@ -171,11 +171,23 @@
             local_sem.at[3 + group],
         )
 
-    def route(group):
+    cuts = full_width // COLUMNS
+
+    def route_first(group):
         part = group_rows(group)
         tail = blocks[part, pl.ds(full_width - TAIL, TAIL)].astype(jnp.float32)
         sel = one_hots(tail, z, top_count)
         sel_ref[part, :] = sel
+        pick_rows(group, sel, 0, cuts // 2)
+
+    def route_rest(group):
+        pick_rows(group, sel_ref[group_rows(group), :], cuts // 2, cuts)
+        for k in range(NX - 1):
+            tile_copy(group, k).start()
+        tile_keep(group).start()
+
+    def pick_rows(group, sel, begin, end):
+        part = group_rows(group)
 
         def pick(i, carry):
             cut = pl.ds(pl.multiple_of(i * COLUMNS, 128), COLUMNS)
@@ -183,17 +195,18 @@
             tiles[group, :, :, cut] = picked.reshape(NX, TILE, COLUMNS)
             return carry
 
-        lax.fori_loop(0, full_width // COLUMNS, pick, 0)
-        for k in range(NX - 1):
-            tile_copy(group, k).start()
-        tile_keep(group).start()
+        lax.fori_loop(begin, end, pick, 0)
 
     keep = [
         pltpu.make_async_copy(owned[j], filled[j].at[dp], local_sem.at[j]) for j in range(3)
     ]
     lanes = [(way, chunk) for chunk in range(2) for way in range(2)]
+    begun = None
     for step in range(half):
         for way, chunk in lanes:
+            if begun is not None and (way, chunk) == lanes[2]:
+                route_rest(begun)
+                begun = None
             if step > 0:
                 copy(step - 1, way, chunk).wait_recv()
             if step < half - 1 or chunk == way:
@@ -209,7 +222,8 @@
             blocks[pl.ds(0, BLOCK), :] = own_ref[...]
         group = {1: 0, 3: 1, 4: 2, 6: 3, 7: 4}.get(step)
         if group is not None:
-            route(group)
+            route_first(group)
+            begun = group
         j = {2: 0, 4: 1, 5: 2}.get(step)
         if j is not None:
             for k in range(2):
@@ -221,9 +235,11 @@
                 for k in range(2):
                     weight(j, 2 + k).wait_recv()
                     weight(j, 7 + k).start()
+    route_rest(begun)
     for way in range(2):
         copy(half - 1, way, way).wait_recv()
-    route(GROUPS - 1)
+    route_first(GROUPS - 1)
+    route_rest(GROUPS - 1)
     for k in range(2):
         weight(2, 2 + k).wait_recv()
         weight(2, 7 + k).start()
@@ -376,10 +392,13 @@
             local_sem.at[group],
         )
 
-    def add_up(group):
-        for k in range(NX - 1):
-            tile_copy(group, k).wait_recv()
-        tile_keep(group).wait()
+    cuts = full_width // COLUMNS
+
+    def add_up(group, begin=0, end=cuts):
+        if begin == 0:
+            for k in range(NX - 1):
+                tile_copy(group, k).wait_recv()
+            tile_keep(group).wait()
         part = group_rows(group)
         sel = sel_ref[part, :]
 
@@ -391,7 +410,7 @@
             ).astype(jnp.bfloat16)
             return carry
 
-        lax.fori_loop(0, full_width // COLUMNS, spread, 0)
+        lax.fori_loop(begin, end, spread, 0)
 
     def copy(step, way, chunk):
         return pltpu.make_async_remote_copy(
@@ -415,10 +434,12 @@
     add_up(GROUPS - 1)
     lanes = [(way, chunk) for chunk in range(2) for way in range(2)]
     for step in range(half):
-        for way, chunk in sorted(lanes, key=lambda lane: lane[0] != lane[1]):
+        for at, (way, chunk) in enumerate(sorted(lanes, key=lambda lane: lane[0] != lane[1])):
             start = first(way, chunk)
             if step < start:
                 continue
+            if at == 2 and step in (3, 4, 6):
+                add_up({3: 2, 4: 1, 6: 0}[step], 0, cuts // 2)
             distance = half - step
             value = parts[rows_of(distance if way == 0 else -distance, chunk), :]
             if step > start:
@@ -431,7 +452,7 @@
             copy(step, way, chunk).start()
         group = {0: 4, 1: 3, 3: 2, 4: 1, 6: 0}.get(step)
         if group is not None:
-            add_up(group)
+            add_up(group, 0 if step < 3 else cuts // 2)
         if step == 2:
             down_near()
         if step == 5:

time: 170 us -> 171 us (level)
  Pallas kernels: 140 us -> 142 us
where the time goes in v5:
time: 171 us
  Pallas kernels  142 us (83%)
  matrix products  15.3 us (9%)
  local copies, waits for them, and re-layouts  7.06 us (4%)
  other arithmetic  5.79 us (3%)
    pallas_call x1, Pallas kernels, ring_gather(): pl.pallas_call(functools.partial(gather_kernel, nz, ny, top_count), out_s...  74.4 us
    pallas_call x1, Pallas kernels, ring_reduce(): pl.pallas_call(functools.partial(reduce_kernel, nz, ny), out_shape=[jax.S...  67.4 us
    dot_general x3, matrix products, contract_last(): lax.dot_general(left, right, (((1,), (1,)), ((), ())), preferred_element_...  4.84 us
    unnamed x12, local copies, waits for them, and re-layouts  4.18 us
    dot_general x1, matrix products, on_device(): jnp.dot(routed_tokens, w_gate, preferred_element_type=jnp.float32)  3.89 us
    dot_general x1, matrix products, contract_first(): lax.dot_general(left, right, (((0,), (0,)), ((), ())), preferred_element_...  3.56 us

profile of v5, /device:TPU:24, one launch (start us, length us, event | category | flops | bytes accessed | tf_op | source)
XLA Modules:
  0.0 170.8 jit_solution(1044798549006900659)
XLA Ops:
  0.6 0.7 convert_element_type.58
  1.3 0.7 reduce_precision.12
  2.0 0.1 copy.24
  2.1 0.1 copy.21
  2.2 0.8 copy.22
  3.0 0.1 fusion.24
  3.0 1.7 pad_maximum_fusion.own_ref
  4.7 74.4 %shard_map.102 = (bf16[4,96,4224]{2,1,0:T(8,128)(2,1)}, bf16[512,64]{1,0:T(8,128)(2,1)}, bf16[8,256,768]{2,1,0:T(8,128)(2,1)}, bf16[8,256,768]{2,1,0:T(8,128)(2,1)}, bf16[8,256,768]{2,1,0:T(8,128)(2,1)}) custom-call(bf16[32,4224]{1,0:T(8,128)(2,1)} %pad_maximum_fusion.own_ref, bf16[256,768]{1,0:T(8,128)(2,1)} %bitcast.21, bf16[256,768]{1,0:T(8,128)(2,1)} %bitcast.22, ...), custom_call_target="tpu_custom_call" | custom-call | tf_op jit(solution)/shard_map/pallas_call | solution.py:269
  79.2 0.9 slice.53
  80.1 0.1 copy.28
  80.2 0.0 copy-start
  80.3 0.0 copy-start.3
  80.3 3.9 %fusion.7 = f32[384,768]{1,0:T(8,128)S(1)} fusion(bf16[2048,768]{1,0:T(8,128)(2,1)} %bitcast.31, bf16[384,4224]{1,0:T(8,128)(2,1)} %bitcast.25), kind=kOutput, calls=%fused_computation.11 | convolution fusion | flops 1207959552 | bytes 5898240 | tf_op jit(solution)/shard_map/dot_general | solution.py:543
  84.2 0.0 copy-done
  84.2 0.4 copy-done.3
  84.5 0.0 copy-start.1
  84.5 1.4 fusion.3
  86.0 0.5 copy-done.1
  86.4 1.7 multiply_convert_fusion.2
  88.1 1.4 convolution_convert_fusion.1
  89.5 0.0 copy-start.2
  89.5 3.6 %convolution_convert_fusion = bf16[2048,768]{1,0:T(8,128)(2,1)} fusion(bf16[384,768]{1,0:T(8,128)(2,1)S(1)} %get-tuple-element.32, bf16[384,4224]{1,0:T(8,128)(2,1)S(1)} %bitcast.28), kind=kOutput, calls=%fused_computation.2 | convolution fusion | flops 1209532416 | bytes 5308416 | tf_op jit(solution)/shard_map/dot_general | solution.py:31
  93.1 0.0 copy-done.2
  93.1 1.7 %fusion.10 = f32[384,2048]{1,0:T(8,128)S(1)} fusion(bf16[2048,768]{1,0:T(8,128)(2,1)S(1)} %bitcast.32, f32[384,768]{1,0:T(8,128)S(1)} %fusion.7, f32[384,768]{1,0:T(8,128)S(1)} %get-tuple-element.42, f32[384,768]{1,0:T(8,128)S(1)} %fusion.3, f32[384]{0:T(512)S(1)} %get-tuple-element.30), kind=kOutput, calls=%fused_computation.19 | convolution fusion | flops 1211203584 | bytes 9831936 | tf_op jit(solution)/shard_map/dot_general | solution.py:25
  94.8 1.7 add_convert_fusion
  96.6 0.1 copy.26
  96.7 1.8 %fusion.1 = bf16[384,4224]{1,0:T(8,128)(2,1)} fusion(bf16[384,24]{1,0:T(8,128)(2,1)S(1)} %copy.26, bf16[384,2048]{1,0:T(8,128)(2,1)S(1)} %add_convert_fusion, bf16[384,2048]{1,0:T(8,128)(2,1)S(1)} %convolution_convert_fusion.1), kind=kLoop, calls=%fused_computation.3 | loop fusion | flops 12976128 | bytes 6408192 | tf_op jit(solution)/shard_map/concatenate | solution.py:561
  98.5 67.4 %shard_map.103 = (bf16[32,4224]{1,0:T(8,128)(2,1)}, bf16[256,768]{1,0:T(8,128)(2,1)}) custom-call(bf16[4,96,4224]{2,1,0:T(8,128)(2,1)} %bitcast.18, bf16[512,64]{1,0:T(8,128)(2,1)} %get-tuple-element.15.sel_ref, bf16[8,256,768]{2,1,0:T(8,128)(2,1)} %bitcast.19), custom_call_target="tpu_custom_call" | custom-call | tf_op jit(solution)/shard_map/pallas_call | solution.py:483
  165.9 0.7 slice_convert_fusion
  166.6 1.7 fusion.27
  168.2 0.1 slice_add_fusion
  168.3 0.7 copy.27
  169.0 1.8 %copy.30 = bf16[1,256,768]{2,1,0:T(8,128)(2,1)} copy(bf16[1,256,768]{2,1,0:T(8,128)(2,1)} %bitcast.20) | data formatting | bytes 786432
  (5 shorter events, 0.1 us)
Async XLA Ops:
  80.2 3.9 %copy-start = (bf16[4,96,4224]{2,1,0:T(8,128)(2,1)S(1)}, bf16[4,96,4224]{2,1,0:T(8,128)(2,1)}, u32[]{:S(2)}) copy-start(bf16[4,96,4224]{2,1,0:T(8,128)(2,1)} %get-tuple-element.11) | copy-start | bytes 9732100
  80.3 4.3 %copy-start.3 = (bf16[8,256,768]{2,1,0:T(8,128)(2,1)S(1)}, bf16[8,256,768]{2,1,0:T(8,128)(2,1)}, u32[]{:S(2)}) copy-start(bf16[8,256,768]{2,1,0:T(8,128)(2,1)} %get-tuple-element.14) | copy-start | bytes 9437188
  84.5 1.9 %copy-start.1 = (bf16[8,256,768]{2,1,0:T(8,128)(2,1)S(1)}, bf16[8,256,768]{2,1,0:T(8,128)(2,1)}, u32[]{:S(2)}) copy-start(bf16[8,256,768]{2,1,0:T(8,128)(2,1)} %get-tuple-element.13) | copy-start | bytes 9437188
  89.5 3.6 %copy-start.2 = (bf16[8,256,768]{2,1,0:T(8,128)(2,1)S(1)}, bf16[8,256,768]{2,1,0:T(8,128)(2,1)}, u32[]{:S(2)}) copy-start(bf16[8,256,768]{2,1,0:T(8,128)(2,1)} %get-tuple-element.12) | copy-start | bytes 9437188
